TPU v7x, 32 devices: a whole 2x2x4 slice. The times are simulated.
32 devices in a mesh: ctx: 8 (over z, y), fsdp: 4 (over x, core).
Axes of the slice: x: 2, y: 2, z: 4, core: 2. Of those that a mesh axis runs over, the one named last changes fastest.
Arguments:
- tokens: bfloat16 [4, 2048, 1024], P('fsdp', 'ctx'), may hold values from -6 to 6
- out_grad: bfloat16 [4, 2048, 1024], P('fsdp', 'ctx'), may hold values from -6 to 6
- lengths: int32 [4, 1], P('fsdp'), may hold values from 512 to 2048, as said below
- norm1_gain: bfloat16 [1024], P('fsdp'), may hold values from 0.5 to 1.5
- w_query: bfloat16 [1024, 1024], P('fsdp'), may hold values from -0.1875 to 0.1875
- w_latent: bfloat16 [1024, 512], P('fsdp'), may hold values from -0.1875 to 0.1875
- w_key_up: bfloat16 [1024, 256], P('fsdp'), may hold values from -0.75 to 0.75
- w_value_up: bfloat16 [1024, 256], P('fsdp'), may hold values from -0.375 to 0.375
- w_output: bfloat16 [1024, 1024], P('fsdp'), may hold values from -1.5 to 1.5
- norm2_gain: bfloat16 [1024], P('fsdp'), may hold values from 0.5 to 1.5
- w_gate: bfloat16 [1024, 2816], P(None, 'fsdp'), may hold values from -0.1875 to 0.1875
- w_up: bfloat16 [1024, 2816], P(None, 'fsdp'), may hold values from -0.1875 to 0.1875
- w_down: bfloat16 [2816, 1024], P('fsdp'), may hold values from -0.109375 to 0.109375
Outputs:
- result: bfloat16 [4, 2048, 1024], P('fsdp', 'ctx')
- token_grad: float32 [4, 2048, 1024], P('fsdp', 'ctx')
- norm1_gain_grad: float32 [1024], P('fsdp')
- w_query_grad: float32 [1024, 1024], P('fsdp')
- w_latent_grad: float32 [1024, 512], P('fsdp')
- w_key_up_grad: float32 [1024, 256], P('fsdp')
- w_value_up_grad: float32 [1024, 256], P('fsdp')
- w_output_grad: float32 [1024, 1024], P('fsdp')
- norm2_gain_grad: float32 [1024], P('fsdp')
- w_gate_grad: float32 [1024, 2816], P(None, 'fsdp')
- w_up_grad: float32 [1024, 2816], P(None, 'fsdp')
- w_down_grad: float32 [2816, 1024], P('fsdp')
Inputs may be any that keep to these rules, and one draw needn't show every extreme that they name: lengths[g, j] valid tokens stand at the start of slot j of group g; the rest of the slot of 2048 rows is padding.
All inputs are finite; a program needn't handle non-finite values.
Results may differ from a plain program's by a relative error of at most 0.025.
Values may be sent and summed in bfloat16 or wider, within the bound.
No kernel may reach another device: no remote copies, remote signals or barrier semaphores. Data moves between devices by JAX's collectives and lax.ppermute only.
A program may use at most 192 MiB of HBM per device.

v0:
```python
import jax
import jax.numpy as jnp
from jax import lax
from jax.sharding import PartitionSpec as P

NH = 16
HD = 64
LAT = 256
GRP = 2
SEQ_MAX = 4096


EPS = 1e-06
NEGATIVE = -1e30


def norm_scale(values):
    return lax.rsqrt(jnp.mean(values * values, axis=-1, keepdims=True) + EPS)


def norm_back(grad_in, normed, scale_rows, gain_full):
    scaled = grad_in * gain_full
    return scale_rows * (scaled - normed * jnp.mean(scaled * normed, axis=-1, keepdims=True))


def key_mask(key_start, key_rows, slot_start, query_pos, length):
    relative = key_start - slot_start + jnp.arange(key_rows, dtype=jnp.int32)
    return (
        (relative[None, :] >= 0)
        & (relative[None, :] <= query_pos[:, None])
        & (relative[None, :] < length)
    )


def raw_scores(query_groups, key_piece, allowed, score_scale):
    grouped = key_piece.reshape(key_piece.shape[0], GRP, LAT)
    scores = (
        jnp.einsum("gpql,kgl->gpqk", query_groups, grouped, preferred_element_type=jnp.float32)
        * score_scale
    )
    return (jnp.where(allowed[None, None], scores, NEGATIVE), grouped)


def on_device(
    tokens,
    out_grad,
    lengths,
    norm1_gain,
    w_query,
    w_latent,
    w_key_up,
    w_value_up,
    w_output,
    norm2_gain,
    w_gate,
    w_up,
    w_down,
):
    ctx_size = lax.axis_size("ctx")
    tok_rows = tokens.shape[1]
    group_rows = tok_rows * ctx_size
    seq_rows = min(SEQ_MAX, group_rows)
    slot_blocks = seq_rows // tok_rows
    head_groups = NH // GRP
    lat_width = GRP * LAT
    my_start = lax.axis_index("ctx") * tok_rows
    slot_number = my_start // seq_rows
    slot_start = slot_number * seq_rows
    length = jnp.sum(
        jnp.where(jnp.arange(lengths.shape[1], dtype=jnp.int32) == slot_number, lengths[0], 0)
    )
    query_pos = my_start - slot_start + jnp.arange(tok_rows, dtype=jnp.int32)
    row_valid = (query_pos < length).astype(jnp.float32)[:, None]
    score_scale = HD ** (-0.5)
    gain_one, query_full, latent_full, key_full, value_full, output_full = (
        lax.all_gather(norm1_gain, "fsdp", axis=0, tiled=True),
        lax.all_gather(w_query, "fsdp", axis=0, tiled=True),
        lax.all_gather(w_latent, "fsdp", axis=0, tiled=True),
        lax.all_gather(w_key_up, "fsdp", axis=0, tiled=True),
        lax.all_gather(w_value_up, "fsdp", axis=0, tiled=True),
        lax.all_gather(w_output, "fsdp", axis=0, tiled=True),
    )
    gain_two, gate_full, up_full, down_full = (
        lax.all_gather(norm2_gain, "fsdp", axis=0, tiled=True),
        lax.all_gather(w_gate, "fsdp", axis=1, tiled=True),
        lax.all_gather(w_up, "fsdp", axis=1, tiled=True),
        lax.all_gather(w_down, "fsdp", axis=0, tiled=True),
    )
    gain_one_f = gain_one.astype(jnp.float32)
    gain_two_f = gain_two.astype(jnp.float32)
    inputs = tokens[0].astype(jnp.float32)
    scale_one = norm_scale(inputs)
    normed_one = inputs * scale_one
    normed = (normed_one * gain_one_f).astype(jnp.bfloat16)
    queries = jnp.dot(normed, query_full, preferred_element_type=jnp.float32).astype(jnp.bfloat16)
    latent = jnp.dot(normed, latent_full, preferred_element_type=jnp.float32).astype(jnp.bfloat16)
    key_heads = key_full.reshape(NH, HD, LAT)
    query_latent = jnp.einsum(
        "shd,hdl->hsl",
        queries.reshape(tok_rows, NH, HD),
        key_heads,
        preferred_element_type=jnp.float32,
    ).astype(jnp.bfloat16)
    query_groups = query_latent.reshape(GRP, head_groups, tok_rows, LAT)

    def is_needed(key_start, key_rows):
        return (
            (key_start + key_rows > slot_start)
            & (key_start < slot_start + length)
            & (key_start < my_start + tok_rows)
        )

    def forward_update(state_now, key_piece, key_start):
        best_now, weight_sum, accum_now = state_now
        allowed = key_mask(key_start, key_piece.shape[0], slot_start, query_pos, length)
        scores, grouped = raw_scores(query_groups, key_piece, allowed, score_scale)
        best_next = jnp.maximum(best_now, jnp.max(scores, axis=-1))
        factor = jnp.exp(best_now - best_next)
        weights = jnp.where(allowed[None, None], jnp.exp(scores - best_next[..., None]), 0.0)
        weight_sum = weight_sum * factor + jnp.sum(weights, axis=-1)
        accum_now = accum_now * factor[..., None] + jnp.einsum(
            "gpqk,kgl->gpql",
            weights.astype(jnp.bfloat16),
            grouped,
            preferred_element_type=jnp.float32,
        )
        return (best_next, weight_sum, accum_now)

    def guarded_forward(state_now, key_piece, key_start):
        return lax.cond(
            is_needed(key_start, key_piece.shape[0]),
            lambda state_in: forward_update(state_in, key_piece, key_start),
            lambda state_in: state_in,
            state_now,
        )

    start_state = (
        jnp.full((GRP, head_groups, tok_rows), NEGATIVE, jnp.float32),
        jnp.zeros((GRP, head_groups, tok_rows), jnp.float32),
        jnp.zeros((GRP, head_groups, tok_rows, LAT), jnp.float32),
    )
    group_latent = lax.all_gather(latent, "ctx", axis=0, tiled=True)

    def forward_loop(block_index, state_now):
        key_start = slot_start + block_index * tok_rows
        key_piece = lax.dynamic_slice_in_dim(group_latent, key_start, tok_rows, 0)
        return guarded_forward(state_now, key_piece, key_start)

    final_state = lax.fori_loop(0, slot_blocks, forward_loop, start_state)
    best_final, sum_final, accum_final = final_state
    log_total = best_final + jnp.log(sum_final)
    mixture = accum_final / sum_final[..., None]
    mixture_low = mixture.astype(jnp.bfloat16)
    value_heads = value_full.reshape(NH, HD, LAT)
    attended = (
        jnp.einsum(
            "hsl,hdl->shd",
            mixture_low.reshape(NH, tok_rows, LAT),
            value_heads,
            preferred_element_type=jnp.float32,
        )
        .reshape(tok_rows, NH * HD)
        .astype(jnp.bfloat16)
    )
    branch = jnp.dot(attended, output_full, preferred_element_type=jnp.float32)
    middle = inputs + branch
    scale_two = norm_scale(middle)
    normed_two_raw = middle * scale_two
    normed_two = (normed_two_raw * gain_two_f).astype(jnp.bfloat16)
    gate_value = jnp.dot(normed_two, gate_full, preferred_element_type=jnp.float32)
    upward = jnp.dot(normed_two, up_full, preferred_element_type=jnp.float32)
    sigmoid_gate = jax.nn.sigmoid(gate_value)
    silu_gate = gate_value * sigmoid_gate
    hidden = (silu_gate * upward).astype(jnp.bfloat16)
    feed_out = jnp.dot(hidden, down_full, preferred_element_type=jnp.float32)
    result = ((middle + feed_out) * row_valid).astype(jnp.bfloat16)
    cotangent = out_grad[0].astype(jnp.float32) * row_valid
    feed_grad = cotangent.astype(jnp.bfloat16)
    down_grad = jnp.einsum("tf,td->fd", hidden, feed_grad, preferred_element_type=jnp.float32)
    hidden_grad = jnp.einsum("td,fd->tf", feed_grad, down_full, preferred_element_type=jnp.float32)
    gate_grad = (
        hidden_grad * upward * sigmoid_gate * (1.0 + gate_value * (1.0 - sigmoid_gate))
    ).astype(jnp.bfloat16)
    up_grad_in = (hidden_grad * silu_gate).astype(jnp.bfloat16)
    gate_w_grad = jnp.einsum("td,tf->df", normed_two, gate_grad, preferred_element_type=jnp.float32)
    up_w_grad = jnp.einsum("td,tf->df", normed_two, up_grad_in, preferred_element_type=jnp.float32)
    normed_two_grad = jnp.einsum(
        "tf,df->td", gate_grad, gate_full, preferred_element_type=jnp.float32
    ) + jnp.einsum("tf,df->td", up_grad_in, up_full, preferred_element_type=jnp.float32)
    gain_two_grad = jnp.sum(normed_two_grad * normed_two_raw, axis=0)
    middle_grad = cotangent + norm_back(normed_two_grad, normed_two_raw, scale_two, gain_two_f)
    branch_grad = middle_grad.astype(jnp.bfloat16)
    output_grad = jnp.einsum("tk,td->kd", attended, branch_grad, preferred_element_type=jnp.float32)
    attended_grad = jnp.einsum(
        "td,kd->tk", branch_grad, output_full, preferred_element_type=jnp.float32
    ).astype(jnp.bfloat16)
    attended_heads = attended_grad.reshape(tok_rows, NH, HD)
    value_grad = jnp.einsum(
        "shd,hsl->hdl",
        attended_heads,
        mixture_low.reshape(NH, tok_rows, LAT),
        preferred_element_type=jnp.float32,
    ).reshape(NH * HD, LAT)
    mixture_grad = (
        jnp.einsum("shd,hdl->hsl", attended_heads, value_heads, preferred_element_type=jnp.float32)
        .astype(jnp.bfloat16)
        .reshape(GRP, head_groups, tok_rows, LAT)
    )
    delta_sum = jnp.sum(mixture_grad * mixture, axis=-1)

    def back_term(query_grad_sum, key_piece, key_start):

        def compute(sum_in):
            allowed = key_mask(key_start, tok_rows, slot_start, query_pos, length)
            scores, grouped = raw_scores(query_groups, key_piece, allowed, score_scale)
            probs = jnp.where(allowed[None, None], jnp.exp(scores - log_total[..., None]), 0.0)
            probs_low = probs.astype(jnp.bfloat16)
            prob_grad = jnp.einsum(
                "gpql,kgl->gpqk", mixture_grad, grouped, preferred_element_type=jnp.float32
            )
            score_grad = (probs * (prob_grad - delta_sum[..., None])).astype(jnp.bfloat16)
            sum_out = sum_in + score_scale * jnp.einsum(
                "gpqk,kgl->gpql", score_grad, grouped, preferred_element_type=jnp.float32
            )
            key_term = score_scale * jnp.einsum(
                "gpqk,gpql->kgl", score_grad, query_groups, preferred_element_type=jnp.float32
            ) + jnp.einsum(
                "gpqk,gpql->kgl", probs_low, mixture_grad, preferred_element_type=jnp.float32
            )
            return (sum_out, key_term.reshape(tok_rows, lat_width))

        def skipped(sum_in):
            return (sum_in, jnp.zeros((tok_rows, lat_width), jnp.float32))

        return lax.cond(is_needed(key_start, tok_rows), compute, skipped, query_grad_sum)

    zero_query = jnp.zeros((GRP, head_groups, tok_rows, LAT), jnp.float32)

    def backward_loop(block_index, state_now):
        sum_now, key_grads = state_now
        key_start = slot_start + block_index * tok_rows
        key_piece = lax.dynamic_slice_in_dim(group_latent, key_start, tok_rows, 0)
        sum_now, key_term = back_term(sum_now, key_piece, key_start)
        key_grads = lax.dynamic_update_slice_in_dim(key_grads, key_term, block_index * tok_rows, 0)
        return (sum_now, key_grads)

    back_start = (zero_query, jnp.zeros((seq_rows, lat_width), jnp.float32))
    query_lat_grad, slot_key_grads = lax.fori_loop(0, slot_blocks, backward_loop, back_start)
    row_count = tok_rows * lax.axis_size("ctx")
    padding = jnp.zeros((row_count, lat_width), jnp.float32)
    padded = jnp.concatenate([padding, slot_key_grads, padding], axis=0)
    offset = jnp.clip(jnp.int32(0) - slot_start + row_count, 0, seq_rows + row_count)
    latent_grad = lax.psum_scatter(
        lax.dynamic_slice_in_dim(padded, offset, row_count, 0).astype(jnp.bfloat16),
        "ctx",
        scatter_dimension=0,
        tiled=True,
    )
    query_lat_low = query_lat_grad.reshape(NH, tok_rows, LAT).astype(jnp.bfloat16)
    key_up_grad = jnp.einsum(
        "shd,hsl->hdl",
        queries.reshape(tok_rows, NH, HD),
        query_lat_low,
        preferred_element_type=jnp.float32,
    ).reshape(NH * HD, LAT)
    query_grad = (
        jnp.einsum("hsl,hdl->shd", query_lat_low, key_heads, preferred_element_type=jnp.float32)
        .reshape(tok_rows, NH * HD)
        .astype(jnp.bfloat16)
    )
    query_w_grad = jnp.einsum("td,tk->dk", normed, query_grad, preferred_element_type=jnp.float32)
    latent_w_grad = jnp.einsum("td,tk->dk", normed, latent_grad, preferred_element_type=jnp.float32)
    normed_grad = jnp.einsum(
        "tk,dk->td", query_grad, query_full, preferred_element_type=jnp.float32
    ) + jnp.einsum("tk,dk->td", latent_grad, latent_full, preferred_element_type=jnp.float32)
    gain_one_grad = jnp.sum(normed_grad * normed_one, axis=0)
    input_grad = middle_grad + norm_back(normed_grad, normed_one, scale_one, gain_one_f)
    shards = (
        lax.psum_scatter(
            gain_one_grad.astype(jnp.bfloat16), "fsdp", scatter_dimension=0, tiled=True
        ).astype(jnp.float32),
        lax.psum_scatter(
            query_w_grad.astype(jnp.bfloat16), "fsdp", scatter_dimension=0, tiled=True
        ).astype(jnp.float32),
        lax.psum_scatter(
            latent_w_grad.astype(jnp.bfloat16), "fsdp", scatter_dimension=0, tiled=True
        ).astype(jnp.float32),
        lax.psum_scatter(
            key_up_grad.astype(jnp.bfloat16), "fsdp", scatter_dimension=0, tiled=True
        ).astype(jnp.float32),
        lax.psum_scatter(
            value_grad.astype(jnp.bfloat16), "fsdp", scatter_dimension=0, tiled=True
        ).astype(jnp.float32),
        lax.psum_scatter(
            output_grad.astype(jnp.bfloat16), "fsdp", scatter_dimension=0, tiled=True
        ).astype(jnp.float32),
        lax.psum_scatter(
            gain_two_grad.astype(jnp.bfloat16), "fsdp", scatter_dimension=0, tiled=True
        ).astype(jnp.float32),
        lax.psum_scatter(
            gate_w_grad.astype(jnp.bfloat16), "fsdp", scatter_dimension=1, tiled=True
        ).astype(jnp.float32),
        lax.psum_scatter(
            up_w_grad.astype(jnp.bfloat16), "fsdp", scatter_dimension=1, tiled=True
        ).astype(jnp.float32),
        lax.psum_scatter(
            down_grad.astype(jnp.bfloat16), "fsdp", scatter_dimension=0, tiled=True
        ).astype(jnp.float32),
    )
    summed = (
        lax.psum(shards[0].astype(jnp.bfloat16), "ctx").astype(jnp.float32),
        lax.psum(shards[1].astype(jnp.bfloat16), "ctx").astype(jnp.float32),
        lax.psum(shards[2].astype(jnp.bfloat16), "ctx").astype(jnp.float32),
        lax.psum(shards[3].astype(jnp.bfloat16), "ctx").astype(jnp.float32),
        lax.psum(shards[4].astype(jnp.bfloat16), "ctx").astype(jnp.float32),
        lax.psum(shards[5].astype(jnp.bfloat16), "ctx").astype(jnp.float32),
        lax.psum(shards[6].astype(jnp.bfloat16), "ctx").astype(jnp.float32),
        lax.psum(shards[7].astype(jnp.bfloat16), "ctx").astype(jnp.float32),
        lax.psum(shards[8].astype(jnp.bfloat16), "ctx").astype(jnp.float32),
        lax.psum(shards[9].astype(jnp.bfloat16), "ctx").astype(jnp.float32),
    )
    return (
        result[None],
        input_grad[None],
        summed[0],
        summed[1],
        summed[2],
        summed[3],
        summed[4],
        summed[5],
        summed[6],
        summed[7],
        summed[8],
        summed[9],
    )


def solution(mesh):
    return jax.shard_map(
        on_device,
        mesh=mesh,
        in_specs=(
            P("fsdp", "ctx", None),
            P("fsdp", "ctx", None),
            P("fsdp", None),
            P("fsdp"),
            P("fsdp", None),
            P("fsdp", None),
            P("fsdp", None),
            P("fsdp", None),
            P("fsdp", None),
            P("fsdp"),
            P(None, "fsdp"),
            P(None, "fsdp"),
            P("fsdp", None),
        ),
        out_specs=(
            P("fsdp", "ctx", None),
            P("fsdp", "ctx", None),
            P("fsdp"),
            P("fsdp", None),
            P("fsdp", None),
            P("fsdp", None),
            P("fsdp", None),
            P("fsdp", None),
            P("fsdp"),
            P(None, "fsdp"),
            P(None, "fsdp"),
            P("fsdp", None),
        ),
        check_vma=False,
    )
```

profile of v0, /device:TPU:0, one launch (start us, length us, event | category | flops | bytes accessed | tf_op | source)
XLA Modules:
  0.0 1037.1 jit_solution(728526672755502800)
XLA Ops:
  9.4 6.0 all-gather
  16.6 12.5 %all-gather.10.cloned.1.call-done = bf16[1024,512]{1,0:T(8,128)(2,1)} async-done(((bf16[256,512]{1,0:T(8,128)(2,1)}), bf16[1024,512]{1,0:T(8,128)(2,1)}) %all-gather.10.cloned.1.call-update) | async-done | bytes 1048592 | tf_op jit(solution)/shard_map/all_gather | solution.py:78
  40.0 10.9 %all_gather.38 = bf16[1024,256]{1,0:T(8,128)(2,1)} all-gather(bf16[256,256]{1,0:T(8,128)(2,1)S(1)} %copy-done.41), channel_id=1, replica_groups=mesh['ctx'=8,'fsdp'=4] {'fsdp'}, dimensions={0}, use_global_device_ids=true | all-gather | bytes 655360 | tf_op jit(solution)/shard_map/all_gather | solution.py:80
  50.9 7.3 all_gather.37
  65.9 42.2 %all-gather.12.cloned.1.call-done = bf16[2048,512]{1,0:T(8,128)(2,1)} async-done(((bf16[256,512]{1,0:T(8,128)(2,1)}), bf16[2048,512]{1,0:T(8,128)(2,1)}) %all-gather.12.cloned.1.call-update) | async-done | bytes 2097168 | tf_op jit(solution)/shard_map/all_gather | solution.py:142
  114.5 10.8 %while.41 = (s32[]{:T(128)}, f32[2,8,256]{2,1,0:T(8,128)S(1)}, f32[2,8,256]{2,1,0:T(8,128)S(1)}, f32[2,8,256,256]{3,2,1,0:T(8,128)}, s32[]{:T(128)}, /*index=5*/...) while((s32[]{:T(128)}, f32[2,8,256]{2,1,0:T(8,128)S(1)}, ...), condition=%wide.region_6.7_spmd.clone, body=%wide.region_1.6_spmd.clone.sunk | while | flops 1089676544 | bytes 58203600 | solution.py:149
  114.5 10.4 %conditional.6 = ((f32[2,8,256]{2,1,0:T(8,128)S(1)}, f32[2,8,256]{2,1,0:T(8,128)S(1)}, f32[2,8,256,256]{3,2,1,0:T(8,128)})) conditional(s32[]{:T(128)} %convert_element_type.380, (f32[2,8,256]{2,1,0:T(8,128)S(1)}, f32[2,8,256]{2,1,0:T(8,128)S(1)}, f32[2,8,256,256]{3,2,1,0:T(8,128)}) %tuple.129, (s32[]{:T(128)}, s32[]{:T(128)}, s32[]{:T(128)}, ...), branch_computations={%region_2.2_spmd, %region_3.5_spmd} | conditional | flops 1089676544 | bytes 58202268 | solution.py:130
  125.2 5.6 copy.71
  139.1 36.4 %all-gather.18.cloned.1.call-done = bf16[1024,2816]{0,1:T(8,128)(2,1)} async-done(((bf16[1024,704]{0,1:T(8,128)(2,1)}), bf16[1024,2816]{0,1:T(8,128)(2,1)}) %all-gather.18.cloned.1.call-update) | async-done | bytes 5767184 | tf_op jit(solution)/shard_map/all_gather | solution.py:85
  175.5 5.9 fusion.79
  181.4 38.9 %all-gather.20.cloned.1.call-done = bf16[1024,2816]{0,1:T(8,128)(2,1)} async-done(((bf16[1024,704]{0,1:T(8,128)(2,1)}), bf16[1024,2816]{0,1:T(8,128)(2,1)}) %all-gather.20.cloned.1.call-update) | async-done | bytes 5767184 | tf_op jit(solution)/shard_map/all_gather | solution.py:86
  220.3 5.9 fusion.80
  226.2 39.1 %all-gather.22.cloned.1.call-done = bf16[2816,1024]{1,0:T(8,128)(2,1)} async-done(((bf16[704,1024]{1,0:T(8,128)(2,1)}), bf16[2816,1024]{1,0:T(8,128)(2,1)}) %all-gather.22.cloned.1.call-update) | async-done | bytes 5767184 | tf_op jit(solution)/shard_map/all_gather | solution.py:87
  265.3 8.2 multiply_convert_fusion
  273.5 5.4 fusion.81
  296.4 20.4 %while.42 = (s32[]{:T(128)}, f32[2,8,256,256]{3,2,1,0:T(8,128)}, bf16[2048,512]{0,1:T(8,128)(2,1)}, s32[]{:T(128)}, s32[]{:T(128)}, /*index=5*/s32[]{:T(128)}, s...) while((s32[]{:T(128)}, f32[2,8,256,256]{3,2,1,0:T(8,128)}, ...), condition=%wide.region_13.14_spmd.clone, body=%wide.region_10.13_spmd.clone.sunk | while | flops 2699625728 | bytes 97771040 | solution.py:248
  296.4 14.2 %conditional.7 = (f32[2,8,256,256]{3,2,1,0:T(8,128)}, bf16[256,512]{0,1:T(8,128)(2,1)S(1)}) conditional(s32[]{:T(128)} %convert_element_type.381, f32[2,8,256,256]{3,2,1,0:T(8,128)} %get-tuple-element.1157, (s32[]{:T(128)}, s32[]{:T(128)}, s32[]{:T(128)}, s32[]{:T(128)}, bf16[2048,512]{0,1:T(8,128)(2,1)}, ...), branch_computations={%region_11.11_spmd, %region_12.12_spmd} | conditional | flops 2699625728 | bytes 97245368 | solution.py:235
  337.7 152.6 %reduce-scatter.10.cloned.1.call-done = bf16[256,512]{0,1:T(8,128)(2,1)} async-done(((bf16[2048,512]{0,1:T(8,128)(2,1)}), bf16[256,512]{0,1:T(8,128)(2,1)}) %reduce-scatter.10.cloned.1.call-update) | async-done | bytes 262160 | tf_op jit(solution)/shard_map/reduce_scatter | solution.py:253
  492.9 5.5 convolution_convert_fusion.2
  498.4 5.7 convolution_convert_fusion.1
  505.5 5.3 convolution_convert_fusion
  513.5 24.2 %reduce-scatter.18.cloned.1.call-done = bf16[256,256]{1,0:T(8,128)(2,1)} async-done(((bf16[1024,256]{1,0:T(8,128)(2,1)}), bf16[256,256]{1,0:T(8,128)(2,1)}) %reduce-scatter.18.cloned.1.call-update) | async-done | bytes 131088 | tf_op jit(solution)/shard_map/reduce_scatter | solution.py:291
  537.7 34.6 %reduce-scatter.12.cloned.1.call-done = bf16[256,1024]{1,0:T(8,128)(2,1)} async-done(((bf16[1024,1024]{1,0:T(8,128)(2,1)}), bf16[256,1024]{1,0:T(8,128)(2,1)}) %reduce-scatter.12.cloned.1.call-update) | async-done | bytes 524304 | tf_op jit(solution)/shard_map/reduce_scatter | solution.py:282
  572.2 34.6 %reduce-scatter.20.cloned.1.call-done = bf16[256,1024]{1,0:T(8,128)(2,1)} async-done(((bf16[1024,1024]{1,0:T(8,128)(2,1)}), bf16[256,1024]{1,0:T(8,128)(2,1)}) %reduce-scatter.20.cloned.1.call-update) | async-done | bytes 524304 | tf_op jit(solution)/shard_map/reduce_scatter | solution.py:294
  606.8 28.0 %reduce-scatter.14.cloned.1.call-done = bf16[256,512]{1,0:T(8,128)(2,1)} async-done(((bf16[1024,512]{1,0:T(8,128)(2,1)}), bf16[256,512]{1,0:T(8,128)(2,1)}) %reduce-scatter.14.cloned.1.call-update) | async-done | bytes 262160 | tf_op jit(solution)/shard_map/reduce_scatter | solution.py:285
  634.8 57.5 %reduce-scatter.22.cloned.1.call-done = bf16[1024,704]{0,1:T(8,128)(2,1)} async-done(((bf16[1024,2816]{0,1:T(8,128)(2,1)}), bf16[1024,704]{0,1:T(8,128)(2,1)}) %reduce-scatter.22.cloned.1.call-update) | async-done | bytes 1441808 | tf_op jit(solution)/shard_map/reduce_scatter | solution.py:300
  692.3 57.3 %reduce-scatter.24.cloned.1.call-done = bf16[1024,704]{0,1:T(8,128)(2,1)} async-done(((bf16[1024,2816]{0,1:T(8,128)(2,1)}), bf16[1024,704]{0,1:T(8,128)(2,1)}) %reduce-scatter.24.cloned.1.call-update) | async-done | bytes 1441808 | tf_op jit(solution)/shard_map/reduce_scatter | solution.py:303
  749.6 57.5 %reduce-scatter.26.cloned.1.call-done = bf16[704,1024]{1,0:T(8,128)(2,1)} async-done(((bf16[2816,1024]{1,0:T(8,128)(2,1)}), bf16[704,1024]{1,0:T(8,128)(2,1)}) %reduce-scatter.26.cloned.1.call-update) | async-done | bytes 1441808 | tf_op jit(solution)/shard_map/reduce_scatter | solution.py:306
  811.4 5.3 fusion.53
  817.5 6.1 all-reduce.4
  823.7 22.1 %all-reduce.2 = (bf16[256]{0:T(256)(128)(2,1)S(1)}, bf16[256]{0:T(256)(128)(2,1)S(1)}) all-reduce(bf16[256]{0:T(256)(128)(2,1)S(1)} %dynamic-slice.1, bf16[256]{0:T(256)(128)(2,1)S(1)} %dynamic-slice.3), channel_id=1, replica_groups=mesh['ctx'=8,'fsdp'=4] {'ctx'}, use_global_device_ids=true, to_apply=%region_18.19 | all-reduce | flops 512 | bytes 2048 | tf_op jit(solution)/shard_map/psum | solution.py:311
  848.2 167.7 %all-reduce.7.cloned.1.call-done = (bf16[256,1024]{1,0:T(8,128)(2,1)}, bf16[256,512]{1,0:T(8,128)(2,1)}, bf16[256,256]{1,0:T(8,128)(2,1)}, bf16[256,256]{1,0:T(8...) async-done(((bf16[256,1024]{1,0:T(8,128)(2,1)}, bf16[256,512]{1,0:T(8,128)(2,1)}, ...) | async-done | bytes 5898256 | tf_op jit(solution)/shard_map/psum | solution.py:312
  (251 shorter events, 132.5 us)
Async XLA Ops:
  7.2 21.8 %all-gather.10.cloned.1.call-start = ((), (), s32[]{:S(2)}) async-start(), calls=%async_computation.9 | async-start | bytes 1310720 | tf_op jit(solution)/shard_map/all_gather | solution.py:78
  7.9 50.3 %all-gather.14.cloned.1.call-start = ((), (), s32[]{:S(2)}) async-start(), calls=%async_computation.11 | async-start | bytes 2621440 | tf_op jit(solution)/shard_map/all_gather | solution.py:77
  8.7 99.4 %all-gather.12.cloned.1.call-start = ((), (), s32[]{:S(2)}) async-start(), calls=%async_computation.10 | async-start | bytes 2359296 | tf_op jit(solution)/shard_map/all_gather | solution.py:142
  31.6 8.4 copy-start.41
  31.6 19.3 %copy-start.42 = (bf16[256,256]{1,0:T(8,128)(2,1)S(1)}, bf16[256,256]{1,0:T(8,128)(2,1)}, u32[]{:S(2)}) copy-start(bf16[256,256]{1,0:T(8,128)(2,1)} %param.27) | copy-start | bytes 393220
  31.6 103.7 %all-gather.16.cloned.1.call-start = ((), (), s32[]{:S(2)}) async-start(), calls=%async_computation.12 | async-start | bytes 2621440 | tf_op jit(solution)/shard_map/all_gather | solution.py:81
  32.2 26.0 %copy-start.8 = (bf16[1,256,1024]{2,1,0:T(8,128)(2,1)S(1)}, bf16[1,256,1024]{2,1,0:T(8,128)(2,1)}, u32[]{:S(2)}) copy-start(bf16[1,256,1024]{2,1,0:T(8,128)(2,1)} %param.21) | copy-start | bytes 1572868
  32.2 143.2 %all-gather.18.cloned.1.call-start = ((), (), s32[]{:S(2)}) async-start(), calls=%async_computation.13 | async-start | bytes 7208960 | tf_op jit(solution)/shard_map/all_gather | solution.py:85
  32.8 187.5 %all-gather.20.cloned.1.call-start = ((), (), s32[]{:S(2)}) async-start(), calls=%async_computation.14 | async-start | bytes 7208960 | tf_op jit(solution)/shard_map/all_gather | solution.py:86
  33.4 231.9 %all-gather.22.cloned.1.call-start = ((), (), s32[]{:S(2)}) async-start(), calls=%async_computation.15 | async-start | bytes 7208960 | tf_op jit(solution)/shard_map/all_gather | solution.py:87
  34.1 456.1 %reduce-scatter.10.cloned.1.call-start = ((), (), s32[]{:S(2)}) async-start(), calls=%async_computation.16 | async-start | bytes 2359296 | tf_op jit(solution)/shard_map/reduce_scatter | solution.py:253
  58.2 4.8 copy-start.22
  139.0 81.3 %copy-start.18 = (bf16[256,1024]{1,0:T(8,128)(2,1)}, bf16[256,1024]{1,0:T(8,128)(2,1)S(1)}, u32[]{:S(2)}) copy-start(bf16[256,1024]{1,0:T(8,128)(2,1)S(1)} %multiply_convert_fusion.3) | copy-start | bytes 1572868
  273.5 5.4 copy-start.34
  273.5 5.4 copy-start.33
  273.5 5.4 copy-start.12
  273.5 5.7 copy-start.43
  322.7 190.8 %reduce-scatter.16.cloned.1.call-start = ((), (), s32[]{:S(2)}) async-start(), calls=%async_computation.19 | async-start | bytes 655360 | tf_op jit(solution)/shard_map/reduce_scatter | solution.py:288
  327.9 209.8 %reduce-scatter.18.cloned.1.call-start = ((), (), s32[]{:S(2)}) async-start(), calls=%async_computation.20 | async-start | bytes 655360 | tf_op jit(solution)/shard_map/reduce_scatter | solution.py:291
  330.6 241.6 %reduce-scatter.12.cloned.1.call-start = ((), (), s32[]{:S(2)}) async-start(), calls=%async_computation.17 | async-start | bytes 2621440 | tf_op jit(solution)/shard_map/reduce_scatter | solution.py:282
  333.0 4.6 copy-start.26
  335.3 271.5 %reduce-scatter.20.cloned.1.call-start = ((), (), s32[]{:S(2)}) async-start(), calls=%async_computation.21 | async-start | bytes 2621440 | tf_op jit(solution)/shard_map/reduce_scatter | solution.py:294
  337.6 155.3 %copy-start.19 = (bf16[256,1024]{1,0:T(8,128)(2,1)S(1)}, bf16[256,1024]{1,0:T(8,128)(2,1)}, u32[]{:S(2)}) copy-start(bf16[256,1024]{1,0:T(8,128)(2,1)} %copy-done.18) | copy-start | bytes 1572868
  337.6 297.2 %reduce-scatter.14.cloned.1.call-start = ((), (), s32[]{:S(2)}) async-start(), calls=%async_computation.18 | async-start | bytes 1310720 | tf_op jit(solution)/shard_map/reduce_scatter | solution.py:285
  492.8 199.4 %reduce-scatter.22.cloned.1.call-start = ((), (), s32[]{:S(2)}) async-start(), calls=%async_computation.22 | async-start | bytes 7208960 | tf_op jit(solution)/shard_map/reduce_scatter | solution.py:300
  498.4 251.2 %reduce-scatter.24.cloned.1.call-start = ((), (), s32[]{:S(2)}) async-start(), calls=%async_computation.23 | async-start | bytes 7208960 | tf_op jit(solution)/shard_map/reduce_scatter | solution.py:303
  504.2 302.8 %reduce-scatter.26.cloned.1.call-start = ((), (), s32[]{:S(2)}) async-start(), calls=%async_computation.24 | async-start | bytes 7208960 | tf_op jit(solution)/shard_map/reduce_scatter | solution.py:306
  510.8 505.1 %all-reduce.7.cloned.1.call-start = ((), (), s32[]{:S(2)}) async-start(), calls=%async_computation.25 | async-start | bytes 11796480 | tf_op jit(solution)/shard_map/psum | solution.py:312
  811.4 5.3 copy-start.38
  811.4 5.3 copy-start.39
  1015.9 7.3 copy-start.40
  1015.9 8.4 copy-start.37
  (31 other events, 75.4 us)
Sparse Core Ops, SparseCore 0:
  9.6 19.4 all-gather.9
  30.6 25.3 all-gather.13
  58.7 49.3 all-gather.11
  109.5 21.0 all-gather.15
  132.0 43.3 all-gather.17
  176.9 43.3 all-gather.19
  221.9 43.3 all-gather.21
  322.8 167.4 reduce-scatter.9
  492.8 20.6 reduce-scatter.15
  516.0 21.6 reduce-scatter.17
  540.8 31.4 reduce-scatter.11
  575.3 31.3 reduce-scatter.19
  609.9 24.8 reduce-scatter.13
  637.3 54.8 reduce-scatter.21
  694.6 54.8 reduce-scatter.23
  752.1 54.8 reduce-scatter.25
  811.5 204.3 all-reduce.6
where the time goes:
time: 1050 us; the launch traced here: 1040 us
  waiting for transfers between devices  789 us (75%)
  matrix products  94.2 us (9%)
  blocking collectives  57.4 us (5%)
  local copies, waits for them, and re-layouts  45.2 us (4%)
  other arithmetic  33 us (3%)
  between operations  16.2 us (2%)
    psum x1, waiting for transfers between devices, on_device(): lax.psum(shards[1].astype(jnp.bfloat16), 'ctx').astype(jnp.float32)  168 us
    reduce_scatter x1, waiting for transfers between devices, on_device(): lax.psum_scatter(lax.dynamic_slice_in_dim(padded, offset, row_count, 0).a...  153 us
    reduce_scatter x1, waiting for transfers between devices, on_device(): lax.psum_scatter(down_grad.astype(jnp.bfloat16), 'fsdp', scatter_dimensio...  57.5 us
    reduce_scatter x1, waiting for transfers between devices, on_device(): lax.psum_scatter(gate_w_grad.astype(jnp.bfloat16), 'fsdp', scatter_dimens...  57.5 us
    reduce_scatter x1, waiting for transfers between devices, on_device(): lax.psum_scatter(up_w_grad.astype(jnp.bfloat16), 'fsdp', scatter_dimensio...  57.3 us
    all_gather x1, waiting for transfers between devices, on_device(): group_latent = lax.all_gather(latent, 'ctx', axis=0, tiled=True)  42.2 us
    all_gather x1, waiting for transfers between devices, on_device(): lax.all_gather(w_down, 'fsdp', axis=0, tiled=True)  39.1 us
    all_gather x1, waiting for transfers between devices, on_device(): lax.all_gather(w_up, 'fsdp', axis=1, tiled=True)  38.9 us
  transfers between devices with their start and end apart: 17, of which 15 were waited for; matrix products, arithmetic and copies ran while one was open for 9% of the time, Pallas kernels for 0%

commit v1 on v0

v1 whole, which is shorter than its diff:
```python
import functools

import jax
import jax.numpy as jnp
from jax import lax
from jax.experimental import pallas as pl
from jax.experimental.pallas import tpu as pltpu
from jax.sharding import PartitionSpec as P

NH = 16
HD = 64
LAT = 256
GRP = 2
SEQ_MAX = 4096
EPS = 1e-06
NEGATIVE = -1e30
HPG = NH // GRP
HB = 2
ORDER = (0, 2, 1, 3)
F32 = jnp.float32
BF16 = jnp.bfloat16


def dot(left, right, contract=((1,), (0,))):
    return lax.dot_general(left, right, (contract, ((), ())), preferred_element_type=F32)


def norm_scale(values):
    return lax.rsqrt(jnp.mean(values * values, axis=-1, keepdims=True) + EPS)


def norm_back(grad_in, normed, scale_rows, gain_full):
    scaled = grad_in * gain_full
    return scale_rows * (scaled - normed * jnp.mean(scaled * normed, axis=-1, keepdims=True))


def swap(value, axis, mask):
    size = lax.axis_size(axis)
    return lax.ppermute(value, axis, [(s, s ^ mask) for s in range(size)])


def gather_four(value):
    across = swap(value, "fsdp", 2)
    beside = swap(value, "fsdp", 1)
    both = swap(across, "fsdp", 1)
    return [value, across, beside, both]


def scatter_four(first_two, last_two):
    got = swap(last_two, "fsdp", 1)
    near = first_two.astype(F32) + got.astype(F32)
    far = swap(near[1].astype(BF16), "fsdp", 2)
    return near[0] + far.astype(F32)


def ring_members(count):
    return list(range(0, count, 2)) + list(range(count - 1, 0, -2)) if count > 1 else [0]


def ring_shift(value, slot_blocks, step):
    size = lax.axis_size("ctx")
    order = ring_members(slot_blocks)
    pairs = []
    for base in range(0, size, slot_blocks):
        for place in range(slot_blocks):
            pairs.append((base + order[place], base + order[(place + step) % slot_blocks]))
    return lax.ppermute(value, "ctx", pairs)


def ring_gather(block, slot_blocks):
    rows = block.shape[0]
    half = slot_blocks // 2
    out = [block]
    from_left, from_right = block, block
    for _ in range(half - 1):
        from_left = ring_shift(from_left, slot_blocks, 1)
        from_right = ring_shift(from_right, slot_blocks, -1)
        out += [from_left, from_right]
    top = ring_shift(from_left[: rows // 2], slot_blocks, 1)
    low = ring_shift(from_right[rows // 2 :], slot_blocks, -1)
    out.append(jnp.concatenate([top, low], axis=0))
    return out


def ring_scatter(terms, slot_blocks):
    rows = terms.shape[1]
    half = slot_blocks // 2
    zero = jnp.zeros((rows // 2, terms.shape[2]), F32)
    last = terms[slot_blocks - 1]
    right = ring_shift(last[: rows // 2], slot_blocks, 1).astype(F32)
    left = ring_shift(last[rows // 2 :], slot_blocks, -1).astype(F32)
    right = jnp.concatenate([right, zero], axis=0)
    left = jnp.concatenate([zero, left], axis=0)
    for k in range(half - 1, 0, -1):
        right = (right + terms[2 * k].astype(F32)).astype(BF16)
        left = (left + terms[2 * k - 1].astype(F32)).astype(BF16)
        right = ring_shift(right, slot_blocks, 1).astype(F32)
        left = ring_shift(left, slot_blocks, -1).astype(F32)
    return terms[0].astype(F32) + right + left


def sum_over_ctx(value, order):
    me = lax.axis_index("ctx")
    cur = value
    for bit in order:
        mine = (me >> bit) & 1
        pair = cur.reshape((2, cur.shape[0] // 2) + cur.shape[1:])
        send = lax.dynamic_index_in_dim(pair, 1 - mine, 0, keepdims=False)
        keep = lax.dynamic_index_in_dim(pair, mine, 0, keepdims=False)
        got = swap(send, "ctx", 1 << bit)
        cur = (keep.astype(F32) + got.astype(F32)).astype(BF16)
    for bit in reversed(order):
        mine = (me >> bit) & 1
        got = swap(cur, "ctx", 1 << bit)
        pair = jnp.zeros((2,) + cur.shape, BF16)
        pair = lax.dynamic_update_index_in_dim(pair, cur, mine, 0)
        pair = lax.dynamic_update_index_in_dim(pair, got, 1 - mine, 0)
        cur = pair.reshape((2 * cur.shape[0],) + cur.shape[1:])
    return cur


def place_of(rank, slots):
    return jnp.where(rank % 2 == 0, rank // 2, slots - 1 - rank // 2)


def member_at(place, slots):
    place = lax.rem(place + slots, slots)
    return jnp.where(place < slots // 2, 2 * place, 2 * (slots - 1 - place) + 1)


def block_start(rank, slot, slots, rows):
    steps = (slot + 1) // 2
    signed = jnp.where(slot % 2 == 1, -steps, steps)
    return member_at(place_of(rank, slots) + signed, slots) * rows


def score_mask(first_key, first_query, length, rows, width):
    key = first_key + lax.broadcasted_iota(jnp.int32, (rows, width), 0)
    query = first_query + lax.rem(lax.broadcasted_iota(jnp.int32, (rows, width), 1), rows)
    return (key <= query) & (key < length)


def forward_kernel(slots, meta, q_ref, wk_ref, wv_ref, c_ref, att_ref, ol_ref, lse_ref,
                   ct_ref, ql_ref, m_ref, l_ref, acc_ref):
    rows = q_ref.shape[1]
    rank, length = meta[0], meta[1]
    first_query = rank * rows
    step = pl.program_id(0)

    def needed(start):
        return (start <= first_query) & (start < length) & (first_query < length)

    @pl.when(step % (HPG // HB) == 0)
    def _():
        def turn(slot, carry):
            @pl.when(needed(block_start(rank, slot, slots, rows)))
            def _():
                ct_ref[slot] = c_ref[slot].T
            return carry

        lax.fori_loop(0, slots, turn, 0)

    for i in range(HB):
        part = pl.ds(i * HD, HD)
        latent_q = dot(wk_ref[part, :], q_ref[part, :], ((0,), (0,))).astype(BF16)
        ql_ref[:, i * rows : (i + 1) * rows] = latent_q * jnp.asarray(HD ** -0.5, BF16)
    m_ref[...] = jnp.full_like(m_ref, NEGATIVE)
    l_ref[...] = jnp.zeros_like(l_ref)
    acc_ref[...] = jnp.zeros_like(acc_ref)

    def block(slot, start, masked):
        scores = dot(c_ref[slot], ql_ref[...])
        if masked:
            allowed = score_mask(start, first_query, length, rows, HB * rows)
            scores = jnp.where(allowed, scores, NEGATIVE)
        best = jnp.maximum(m_ref[...], jnp.max(scores, axis=0, keepdims=True))
        weights = jnp.exp(scores - best)
        if masked:
            weights = jnp.where(allowed, weights, 0.0)
        factor = jnp.exp(m_ref[...] - best)
        m_ref[...] = best
        l_ref[...] = l_ref[...] * factor + jnp.sum(weights, axis=0, keepdims=True)
        acc_ref[...] = acc_ref[...] * factor + dot(ct_ref[slot], weights.astype(BF16))

    def loop(slot, carry):
        start = block_start(rank, slot, slots, rows)
        plain = (start + rows <= first_query + 1) & (start + rows <= length)

        @pl.when(needed(start) & plain)
        def _():
            block(slot, start, False)

        @pl.when(needed(start) & jnp.logical_not(plain))
        def _():
            block(slot, start, True)

        return carry

    lax.fori_loop(0, slots, loop, 0)
    total = l_ref[...]
    seen = total > 0.0
    safe = jnp.where(seen, total, 1.0)
    lse_all = jnp.where(seen, m_ref[...] + jnp.log(safe), 0.0)
    mixture = (acc_ref[...] * (1.0 / safe)).astype(BF16)
    for i in range(HB):
        part = pl.ds(i * HD, HD)
        cols = slice(i * rows, (i + 1) * rows)
        lse_ref[i] = lse_all[:, cols]
        ol_ref[i] = mixture[:, cols]
        att_ref[part, :] = dot(wv_ref[part, :], mixture[:, cols]).astype(BF16)


def backward_kernel(slots, meta, q_ref, da_ref, wk_ref, wv_ref, c_ref, ol_ref, lse_ref,
                    dq_ref, dwk_ref, dwv_ref, dc_ref,
                    ct_ref, dc_acc, qlt_ref, dot_ref, both_ref, dql_ref, delta_ref):
    rows = q_ref.shape[1]
    rank, length = meta[0], meta[1]
    first_query = rank * rows
    step = pl.program_id(0)
    steps = HPG // HB
    scale = jnp.asarray(HD ** -0.5, BF16)

    def needed(start):
        return (start <= first_query) & (start < length) & (first_query < length)

    @pl.when(step % steps == 0)
    def _():
        dc_acc[...] = jnp.zeros_like(dc_acc)

        def turn(slot, carry):
            @pl.when(needed(block_start(rank, slot, slots, rows)))
            def _():
                ct_ref[slot] = c_ref[slot].T
            return carry

        lax.fori_loop(0, slots, turn, 0)

    for i in range(HB):
        part = pl.ds(i * HD, HD)
        q_t, da_t, wk, wv = q_ref[part, :], da_ref[part, :], wk_ref[part, :], wv_ref[part, :]
        qlt_ref[i] = dot(wk, q_t, ((0,), (0,))).astype(BF16) * scale
        both_ref[i, :rows] = dot(q_t, wk, ((0,), (0,))).astype(BF16) * scale
        dol_t = dot(wv, da_t, ((0,), (0,))).astype(BF16)
        dot_ref[i] = dol_t
        both_ref[i, rows:] = dot(da_t, wv, ((0,), (0,))).astype(BF16)
        delta_ref[i] = jnp.sum(dol_t.astype(F32) * ol_ref[i].astype(F32), axis=0, keepdims=True)
    dql_ref[...] = jnp.zeros_like(dql_ref)

    def block(slot, start, masked):
        keys = c_ref[slot]
        keys_t = ct_ref[slot]
        if masked:
            allowed = score_mask(start, first_query, length, rows, rows)
        total = dc_acc[slot]
        for i in range(HB):
            scores = dot(keys, qlt_ref[i])
            probs = jnp.exp(scores - lse_ref[i])
            if masked:
                probs = jnp.where(allowed, probs, 0.0)
            grads = dot(keys, dot_ref[i])
            score_grad = (probs * (grads - delta_ref[i])).astype(BF16)
            dql_ref[i] += dot(keys_t, score_grad)
            pair = jnp.concatenate([score_grad, probs.astype(BF16)], axis=1)
            total = total + dot(pair, both_ref[i])
        dc_acc[slot] = total

    def loop(slot, carry):
        start = block_start(rank, slot, slots, rows)
        plain = (start + rows <= first_query + 1) & (start + rows <= length)

        @pl.when(needed(start) & plain)
        def _():
            block(slot, start, False)

        @pl.when(needed(start) & jnp.logical_not(plain))
        def _():
            block(slot, start, True)

        return carry

    lax.fori_loop(0, slots, loop, 0)
    for i in range(HB):
        part = pl.ds(i * HD, HD)
        latent_grad = (dql_ref[i] * (HD ** -0.5)).astype(BF16)
        dq_ref[part, :] = dot(wk_ref[part, :], latent_grad).astype(BF16)
        dwk_ref[part, :] = dot(q_ref[part, :], latent_grad, ((1,), (1,))).astype(BF16)
        dwv_ref[part, :] = dot(da_ref[part, :], ol_ref[i], ((1,), (1,))).astype(BF16)

    @pl.when(step % steps == steps - 1)
    def _():
        dc_ref[...] = dc_acc[...].astype(BF16)


def head_place(step, member):
    per_piece = NH // 4 // HB
    mask = (step // per_piece) ^ member
    return ((mask & 1) * 2 + (mask >> 1)) * per_piece + step % per_piece


def attention_forward(meta, q_t, wk, wv, blocks):
    slots, rows, _ = blocks.shape
    own = lambda s, meta: (s, 0)
    placed = lambda s, meta: (head_place(s, meta[2]), 0)
    width = HB * HD
    return pl.pallas_call(
        functools.partial(forward_kernel, slots),
        name="attention_forward",
        grid_spec=pltpu.PrefetchScalarGridSpec(
            num_scalar_prefetch=1,
            grid=(NH // HB,),
            in_specs=[
                pl.BlockSpec((width, rows), own),
                pl.BlockSpec((width, LAT), placed),
                pl.BlockSpec((width, LAT), placed),
                pl.BlockSpec((slots, rows, LAT), lambda s, meta: (0, 0, s // (HPG // HB))),
            ],
            out_specs=[
                pl.BlockSpec((width, rows), placed),
                pl.BlockSpec((HB, LAT, rows), lambda s, meta: (s, 0, 0)),
                pl.BlockSpec((HB, 1, rows), lambda s, meta: (s, 0, 0)),
            ],
            scratch_shapes=[
                pltpu.VMEM((slots, LAT, rows), BF16),
                pltpu.VMEM((LAT, HB * rows), BF16),
                pltpu.VMEM((1, HB * rows), F32),
                pltpu.VMEM((1, HB * rows), F32),
                pltpu.VMEM((LAT, HB * rows), F32),
            ],
        ),
        out_shape=[
            jax.ShapeDtypeStruct((NH * HD, rows), BF16),
            jax.ShapeDtypeStruct((NH, LAT, rows), BF16),
            jax.ShapeDtypeStruct((NH, 1, rows), F32),
        ],
        compiler_params=pltpu.CompilerParams(
            dimension_semantics=("arbitrary",), vmem_limit_bytes=32 << 20
        ),
    )(meta, q_t, wk, wv, blocks)


def attention_backward(meta, q_t, da_t, wk, wv, blocks, ol, lse):
    slots, rows, _ = blocks.shape
    own = lambda s, meta: (s, 0)
    placed = lambda s, meta: (head_place(s, meta[2]), 0)
    whole = lambda s, meta: (0, 0, s // (HPG // HB))
    width = HB * HD
    return pl.pallas_call(
        functools.partial(backward_kernel, slots),
        name="attention_backward",
        grid_spec=pltpu.PrefetchScalarGridSpec(
            num_scalar_prefetch=1,
            grid=(NH // HB,),
            in_specs=[
                pl.BlockSpec((width, rows), own),
                pl.BlockSpec((width, rows), placed),
                pl.BlockSpec((width, LAT), placed),
                pl.BlockSpec((width, LAT), placed),
                pl.BlockSpec((slots, rows, LAT), whole),
                pl.BlockSpec((HB, LAT, rows), lambda s, meta: (s, 0, 0)),
                pl.BlockSpec((HB, 1, rows), lambda s, meta: (s, 0, 0)),
            ],
            out_specs=[
                pl.BlockSpec((width, rows), own),
                pl.BlockSpec((width, LAT), placed),
                pl.BlockSpec((width, LAT), placed),
                pl.BlockSpec((slots, rows, LAT), whole),
            ],
            scratch_shapes=[
                pltpu.VMEM((slots, LAT, rows), BF16),
                pltpu.VMEM((slots, rows, LAT), F32),
                pltpu.VMEM((HB, LAT, rows), BF16),
                pltpu.VMEM((HB, LAT, rows), BF16),
                pltpu.VMEM((HB, 2 * rows, LAT), BF16),
                pltpu.VMEM((HB, LAT, rows), F32),
                pltpu.VMEM((HB, 1, rows), F32),
            ],
        ),
        out_shape=[
            jax.ShapeDtypeStruct((NH * HD, rows), BF16),
            jax.ShapeDtypeStruct((NH * HD, LAT), BF16),
            jax.ShapeDtypeStruct((NH * HD, LAT), BF16),
            jax.ShapeDtypeStruct(blocks.shape, BF16),
        ],
        compiler_params=pltpu.CompilerParams(
            dimension_semantics=("arbitrary",), vmem_limit_bytes=40 << 20
        ),
    )(meta, q_t, da_t, wk, wv, blocks, ol, lse)


def on_device(
    tokens,
    out_grad,
    lengths,
    norm1_gain,
    w_query,
    w_latent,
    w_key_up,
    w_value_up,
    w_output,
    norm2_gain,
    w_gate,
    w_up,
    w_down,
):
    ctx_size = lax.axis_size("ctx")
    tok_rows, width = tokens.shape[1], tokens.shape[2]
    ff = w_gate.shape[1]
    group_rows = tok_rows * ctx_size
    seq_rows = min(SEQ_MAX, group_rows)
    slots = seq_rows // tok_rows
    ctx_rank = lax.axis_index("ctx")
    member = lax.axis_index("fsdp")
    slot_number = ctx_rank // slots
    rank = ctx_rank % slots
    length = jnp.sum(
        jnp.where(jnp.arange(lengths.shape[1], dtype=jnp.int32) == slot_number, lengths[0], 0)
    )
    meta = jnp.stack([rank, length, member]).astype(jnp.int32)
    query_pos = rank * tok_rows + jnp.arange(tok_rows, dtype=jnp.int32)
    row_valid = (query_pos < length).astype(F32)[:, None]
    piece = width // 4
    bits = ctx_size.bit_length() - 1

    def reorder(value):
        return jnp.concatenate(
            [lax.dynamic_slice_in_dim(value, (member ^ m) * piece, piece, 1) for m in ORDER], axis=1
        )

    def restore(value):
        back = {m: t for t, m in enumerate(ORDER)}
        parts = [value[:, back[m] * piece : (back[m] + 1) * piece] for m in range(4)]
        low = (member & 1) == 1
        parts = [jnp.where(low, parts[j ^ 1], parts[j]) for j in range(4)]
        high = (member & 2) == 2
        parts = [jnp.where(high, parts[j ^ 2], parts[j]) for j in range(4)]
        return jnp.concatenate(parts, axis=1)

    gains = jnp.stack([norm1_gain, norm2_gain])
    gain_pieces = gather_four(gains)
    latent_pieces = gather_four(w_latent)
    gate_order = lax.optimization_barrier((latent_pieces[1], w_query, w_key_up, w_value_up))
    latent_pieces[1] = gate_order[0]
    query_pieces = gather_four(gate_order[1])
    side = jnp.concatenate([gate_order[2], gate_order[3]], axis=1)
    side_pieces = gather_four(side)
    gate_order = lax.optimization_barrier((query_pieces[1], side_pieces[1], w_output))
    query_pieces[1], side_pieces[1] = gate_order[0], gate_order[1]
    output_pieces = gather_four(gate_order[2])
    cotangent = out_grad[0].astype(F32) * row_valid
    gate_order = lax.optimization_barrier((output_pieces[1], cotangent.astype(BF16)))
    output_pieces[1] = gate_order[0]
    feed_grad = jnp.concatenate(gather_four(gate_order[1]), axis=0)

    gain_one = jnp.concatenate([g[0] for g in gain_pieces])
    gain_two = restore(jnp.concatenate([g[1:] for g in gain_pieces], axis=1))
    gain_one_f = gain_one.astype(F32)
    gain_two_f = gain_two.astype(F32)
    query_full = jnp.concatenate(query_pieces, axis=0)
    latent_full = jnp.concatenate(latent_pieces, axis=0)
    side_full = jnp.concatenate(side_pieces, axis=0)
    key_full, value_full = side_full[:, :LAT], side_full[:, LAT:]
    output_full = jnp.concatenate(output_pieces, axis=0)

    inputs = tokens[0].astype(F32)
    mixed = reorder(tokens[0]).astype(F32)
    scale_one = norm_scale(inputs)
    normed_one = mixed * scale_one
    normed = (normed_one * gain_one_f).astype(BF16)
    latent = dot(normed, latent_full).astype(BF16)
    blocks = jnp.stack(ring_gather(latent, slots))
    q_t = dot(query_full, normed, ((0,), (1,))).astype(BF16)
    att_t, mixture, log_total = attention_forward(meta, q_t, key_full, value_full, blocks)
    middle = inputs + dot(att_t, output_full, ((0,), (0,)))
    scale_two = norm_scale(middle)
    normed_two_raw = middle * scale_two
    normed_two = (normed_two_raw * gain_two_f).astype(BF16)
    ff_in = jnp.concatenate(gather_four(normed_two), axis=0)

    gate_value = dot(ff_in, w_gate)
    upward = dot(ff_in, w_up)
    hidden_grad = dot(feed_grad, w_down, ((1,), (1,)))
    sigmoid_gate = jax.nn.sigmoid(gate_value)
    silu_gate = gate_value * sigmoid_gate
    hidden = (silu_gate * upward).astype(BF16)
    gate_grad = (
        hidden_grad * upward * sigmoid_gate * (1.0 + gate_value * (1.0 - sigmoid_gate))
    ).astype(BF16)
    up_grad = (hidden_grad * silu_gate).astype(BF16)
    normed_two_part = (
        dot(gate_grad, w_gate, ((1,), (1,))) + dot(up_grad, w_up, ((1,), (1,)))
    ).astype(BF16).reshape(4, tok_rows, width)
    normed_two_grad = scatter_four(normed_two_part[:2], normed_two_part[2:])
    feed_part = dot(hidden, w_down).astype(BF16).reshape(4, tok_rows, width)
    feed_out = scatter_four(feed_part[:2], feed_part[2:])
    result = ((middle + feed_out) * row_valid).astype(BF16)

    zigzag = list(range(bits))
    other = zigzag[1:2] + zigzag[:1] + zigzag[2:]
    split = lambda v: v.reshape((ctx_size, v.shape[0] // ctx_size) + v.shape[1:])
    join = lambda v: v.reshape((v.shape[0] * v.shape[1],) + v.shape[2:])
    gate_w_part = dot(ff_in, gate_grad, ((0,), (0,))).astype(BF16)
    up_w_part = dot(ff_in, up_grad, ((0,), (0,))).astype(BF16)
    down_part = dot(hidden, feed_grad, ((0,), (0,))).astype(BF16)
    gate_w_grad = join(sum_over_ctx(split(gate_w_part), zigzag)).astype(F32)
    down_grad = join(sum_over_ctx(split(down_part), other)).astype(F32)
    up_w_grad = join(sum_over_ctx(split(up_w_part), zigzag)).astype(F32)

    middle_grad = cotangent + norm_back(normed_two_grad, normed_two_raw, scale_two, gain_two_f)
    branch_grad = middle_grad.astype(BF16)
    da_t = dot(output_full, branch_grad, ((1,), (1,))).astype(BF16)
    dq_t, key_w_part, value_w_part, latent_terms = attention_backward(
        meta, q_t, da_t, key_full, value_full, blocks, mixture, log_total
    )
    latent_grad = ring_scatter(latent_terms, slots).astype(BF16)

    quarter = lambda v: v.reshape((4, v.shape[0] // 4) + v.shape[1:])
    output_part = quarter(dot(att_t, branch_grad).astype(BF16))
    output_shard = scatter_four(output_part[:2], output_part[2:])
    output_grad = join(sum_over_ctx(split(output_shard.astype(BF16)), zigzag)).astype(F32)
    query_part = quarter(dot(normed, dq_t, ((0,), (1,))).astype(BF16))
    query_shard = scatter_four(query_part[:2], query_part[2:])
    query_grad = join(sum_over_ctx(split(query_shard.astype(BF16)), other)).astype(F32)
    latent_w_part = dot(normed, latent_grad, ((0,), (0,))).astype(BF16)
    side_part = quarter(jnp.concatenate([latent_w_part, key_w_part, value_w_part], axis=1))
    side_shard = scatter_four(side_part[:2], side_part[2:])
    side_grad = join(sum_over_ctx(split(side_shard.astype(BF16)), zigzag)).astype(F32)
    lat_width = GRP * LAT
    latent_w_grad = side_grad[:, :lat_width]
    key_grad = side_grad[:, lat_width : lat_width + LAT]
    value_grad = side_grad[:, lat_width + LAT :]

    normed_grad = dot(dq_t, query_full, ((0,), (1,))) + dot(
        latent_grad, latent_full, ((1,), (1,))
    )
    input_grad = middle_grad + restore(
        norm_back(normed_grad, normed_one, scale_one, gain_one_f)
    )
    gain_one_grad = (
        jnp.sum(w_query.astype(F32) * query_grad, axis=1)
        + jnp.sum(w_latent.astype(F32) * latent_w_grad, axis=1)
    ) / norm1_gain.astype(F32)
    gain_two_part = jnp.sum(
        w_gate.astype(F32) * gate_w_grad + w_up.astype(F32) * up_w_grad, axis=1
    ).astype(BF16)
    gain_two_part = reorder(gain_two_part[None]).reshape(4, 1, piece)
    gain_two_grad = scatter_four(gain_two_part[:2], gain_two_part[2:])[0] / norm2_gain.astype(F32)
    return (
        result[None],
        input_grad[None],
        gain_one_grad,
        query_grad,
        latent_w_grad,
        key_grad,
        value_grad,
        output_grad,
        gain_two_grad,
        gate_w_grad,
        up_w_grad,
        down_grad,
    )


def solution(mesh):
    rows = P("fsdp", None)
    cols = P(None, "fsdp")
    toks = P("fsdp", "ctx", None)
    vec = P("fsdp")
    return jax.shard_map(
        on_device,
        mesh=mesh,
        in_specs=(toks, toks, rows, vec, rows, rows, rows, rows, rows, vec, cols, cols, rows),
        out_specs=(toks, toks, vec, rows, rows, rows, rows, rows, vec, cols, cols, rows),
        check_vma=False,
    )
```

time: 1050 us -> 563 us (0.54)
  waiting for transfers between devices: 789 us -> 162 us
  starting transfers between devices: 0.94 us -> 154 us
  local copies, waits for them, and re-layouts: 45.2 us -> 124 us
  blocking collectives: 57.4 us -> 0 us
  matrix products: 94.2 us -> 38 us
  Pallas kernels: 0 us -> 32.3 us
  between operations: 16.2 us -> 3.41 us
    reduce_scatter x9 -> x0, waiting for transfers between devices: 449 us -> none  [the longest x1 153 us: on_device(): lax.psum_scatter(lax.dynamic_slice_in_dim(padded, offset, row_count, 0).a...]
    all_gather x7 -> x0, waiting for transfers between devices: 169 us -> none  [the longest x1 42.2 us: on_device(): group_latent = lax.all_gather(latent, 'ctx', axis=0, tiled=True)]
    psum x1 -> x0, waiting for transfers between devices: 168 us -> none  [on_device(): lax.psum(shards[1].astype(jnp.bfloat16), 'ctx').astype(jnp.float32)]
    ppermute x0 -> x85, waiting for transfers between devices: none -> 162 us  [the longest x69 114 us: swap(): return lax.ppermute(value, axis, [(s, s ^ mask) for s in range(size)])]
    ppermute x0 -> x85, starting transfers between devices: none -> 154 us  [the longest x69 106 us: swap(): return lax.ppermute(value, axis, [(s, s ^ mask) for s in range(size)])]
    dynamic_update_slice x8 -> x32, local copies, waits for them, and re-layouts: 5.81 us -> 63.7 us  [the longest x18 32.3 us: sum_over_ctx(): pair = lax.dynamic_update_index_in_dim(pair, got, 1 - mine, 0)]
    dot_general x31 -> x18, matrix products: 94.2 us -> 38 us  [dot(): lax.dot_general(left, right, (contract, ((), ())), preferred_element_type...]
    pallas_call x0 -> x2, Pallas kernels: none -> 32.3 us  [the longest x1 19.1 us: attention_backward(): pl.pallas_call(functools.partial(backward_kernel, slots), name='attention...]
  transfers between devices with their start and end apart: 17 -> 85, of which waited for: 15 -> 33; matrix products, arithmetic and copies ran while one was open for 9% -> 32% of each run, Pallas kernels for 0% -> 6%
where the time goes in v1:
time: 563 us; the launch traced here: 554 us
  waiting for transfers between devices  162 us (29%)
  starting transfers between devices  154 us (27%)
  local copies, waits for them, and re-layouts  124 us (22%)
  other arithmetic  41.2 us (7%)
  matrix products  38 us (7%)
  Pallas kernels  32.3 us (6%)
    ppermute x69, waiting for transfers between devices, swap(): return lax.ppermute(value, axis, [(s, s ^ mask) for s in range(size)])  114 us
    ppermute x69, starting transfers between devices, swap(): return lax.ppermute(value, axis, [(s, s ^ mask) for s in range(size)])  106 us
    ppermute x16, waiting for transfers between devices, ring_shift(): return lax.ppermute(value, 'ctx', pairs)  47.8 us
    ppermute x16, starting transfers between devices, ring_shift(): return lax.ppermute(value, 'ctx', pairs)  47.5 us
    dot_general x18, matrix products, dot(): lax.dot_general(left, right, (contract, ((), ())), preferred_element_type...  38 us
    dynamic_update_slice x18, local copies, waits for them, and re-layouts, sum_over_ctx(): pair = lax.dynamic_update_index_in_dim(pair, got, 1 - mine, 0)  32.3 us
    dynamic_update_slice x14, local copies, waits for them, and re-layouts, sum_over_ctx(): pair = lax.dynamic_update_index_in_dim(pair, cur, mine, 0)  31.3 us
    pallas_call x1, Pallas kernels, attention_backward(): pl.pallas_call(functools.partial(backward_kernel, slots), name='attention...  19.1 us
  transfers between devices with their start and end apart: 85, of which 33 were waited for; matrix products, arithmetic and copies ran while one was open for 32% of the time, Pallas kernels for 6%

profile of v1, /device:TPU:0, one launch (start us, length us, event | category | flops | bytes accessed | tf_op | source)
XLA Modules:
  0.0 554.5 jit_solution(6527928959688353489)
XLA Ops:
  24.2 10.4 %collective-permute-done.2 = bf16[256,512]{1,0:T(8,128)(2,1)S(1)} collective-permute-done((bf16[256,512]{1,0:T(8,128)(2,1)S(1)}, bf16[256,512]{1,0:T(8,128)(2,1)S(1)}, u32[]{:S(2)}, u32[]{:S(2)}) %collective-permute-start.2) | collective-permute-done | bytes 262176 | tf_op jit(solution)/shard_map/ppermute | solution.py:39
  39.5 6.3 %collective-permute-done.14 = bf16[256,512]{1,0:T(8,128)(2,1)S(1)} collective-permute-done((bf16[256,512]{1,0:T(8,128)(2,1)S(1)}, bf16[256,512]{1,0:T(8,128)(2,1)S(1)}, u32[]{:S(2)}, u32[]{:S(2)}) %collective-permute-start.14) | collective-permute-done | bytes 262176 | tf_op jit(solution)/shard_map/ppermute | solution.py:67
  47.8 7.1 %collective-permute-done.17 = bf16[256,512]{1,0:T(8,128)(2,1)S(1)} collective-permute-done((bf16[256,512]{1,0:T(8,128)(2,1)S(1)}, bf16[256,512]{1,0:T(8,128)(2,1)S(1)}, u32[]{:S(2)}, u32[]{:S(2)}) %collective-permute-start.17) | collective-permute-done | bytes 262176 | tf_op jit(solution)/shard_map/ppermute | solution.py:67
  60.6 13.2 %attention_forward.1 = (bf16[1024,256]{1,0:T(8,128)(2,1)S(1)}, bf16[16,256,256]{2,1,0:T(8,128)(2,1)S(1)}, f32[16,1,256]{2,1,0:T(1,128)S(1)}) custom-call(s32[3]{0:T(128)S(1)} %pad_add_fusion.meta, bf16[1024,256]{1,0:T(8,128)(2,1)S(1)} %convolution_convert_fusion.8.q_ref, bf16[1024,256]{1,0:T(8,128)(2,1)S(1)} %get-tuple-element.93.wk_ref, ...), custom_call_target="tpu_custom_call" | custom-call | tf_op jit(solution)/shard_map/attention_forward/pallas_call | solution.py:305
  78.8 12.2 %collective-permute-done.23 = bf16[256,1024]{1,0:T(8,128)(2,1)} collective-permute-done((bf16[256,1024]{1,0:T(8,128)(2,1)}, bf16[256,1024]{1,0:T(8,128)(2,1)}, u32[]{:S(2)}, u32[]{:S(2)}) %collective-permute-start.23) | collective-permute-done | bytes 524320 | tf_op jit(solution)/shard_map/ppermute | solution.py:39
  116.6 4.4 reshape_reshape.28
  123.2 4.7 collective-permute-start.71
  127.9 4.7 convolution_convert_fusion.4
  144.2 10.2 %collective-permute-start.79 = (bf16[4,88,1024]{2,1,0:T(8,128)(2,1)S(1)}, bf16[4,88,1024]{2,1,0:T(8,128)(2,1)S(1)}, u32[]{:S(2)}, u32[]{:S(2)}) collective-permute-start(bf16[4,88,1024]{2,1,0:T(8,128)(2,1)S(1)} %dynamic-slice_bitcast_fusion), channel_id=1, source_target_pairs={{0,8},{4,12},{8,0},{12,4},{16,24},{20,28},{24,16},{28,20},{1,9},{5... | collective-permute-start | bytes 2162696 | tf_op jit(solution)/shard_map/ppermute | solution.py:39
  160.6 10.2 %collective-permute-start.66 = (bf16[2,128,704]{1,0,2:T(2,128)(2,1)S(1)}, bf16[2,128,704]{1,0,2:T(2,128)(2,1)S(1)}, u32[]{:S(2)}, u32[]{:S(2)}) collective-permute-start(bf16[2,128,704]{1,0,2:T(2,128)(2,1)S(1)} %dynamic-slice_bitcast_fusion.5), channel_id=1, source_target_pairs={{0,8},{4,12},{8,0},{12,4},{16,24},{20,28},{24,16},{28,20},{1,9},{5... | collective-permute-start | bytes 1081352 | tf_op jit(solution)/shard_map/ppermute | solution.py:39
  180.5 17.3 %collective-permute-start.73 = (bf16[1,128,704]{1,0,2:T(2,128)(2,1)S(1)}, bf16[1,128,704]{1,0,2:T(2,128)(2,1)S(1)}, u32[]{:S(2)}, u32[]{:S(2)}) collective-permute-start(bf16[1,128,704]{1,0,2:T(2,128)(2,1)S(1)} %constant_dynamic-slice_fusion.1), channel_id=1, source_target_pairs={{0,16},{4,20},{8,24},{12,28},{16,0},{20,4},{24,8},{28,12},{1,17},{... | collective-permute-start | bytes 540680 | tf_op jit(solution)/shard_map/ppermute | solution.py:39
  199.3 6.2 %collective-permute-start.67 = (bf16[1,128,704]{1,0,2:T(2,128)(2,1)}, bf16[1,128,704]{1,0,2:T(2,128)(2,1)}, u32[]{:S(2)}, u32[]{:S(2)}) collective-permute-start(bf16[1,128,704]{1,0,2:T(2,128)(2,1)} %constant_dynamic-slice_fusion.2), channel_id=1, source_target_pairs={{0,16},{4,20},{8,24},{12,28},{16,0},{20,4},{24,8},{28,12},{1,17},{... | collective-permute-start | bytes 540680 | tf_op jit(solution)/shard_map/ppermute | solution.py:39
  206.3 20.1 %collective-permute-done.73 = bf16[1,128,704]{1,0,2:T(2,128)(2,1)S(1)} collective-permute-done((bf16[1,128,704]{1,0,2:T(2,128)(2,1)S(1)}, bf16[1,128,704]{1,0,2:T(2,128)(2,1)S(1)}, u32[]{:S(2)}, u32[]{:S(2)}) %collective-permute-start.73) | collective-permute-done | bytes 180256 | tf_op jit(solution)/shard_map/ppermute | solution.py:39
  227.9 9.2 %dynamic_update_slice.153 = bf16[2,128,704]{1,0,2:T(2,128)(2,1)} dynamic-update-slice(bf16[2,128,704]{1,0,2:T(2,128)(2,1)} %reshape.382.clone, bf16[1,128,704]{1,0,2:T(2,128)(2,1)S(1)} %add_convert_fusion.2, s32[]{:T(128)S(6)} %select_n.240, s32[]{:T(128)} %constant.255.clone.1, s32[]{:T(128)} %constant.255.clone.1) | dynamic-update-slice | bytes 360452 | tf_op jit(solution)/shard_map/jit(dynamic_update_index_in_dim)/dynamic_update_slice | solution.py:116
  237.2 4.8 collective-permute-done.67
  244.5 9.2 %dynamic_update_slice.147 = bf16[2,128,704]{1,0,2:T(2,128)(2,1)} dynamic-update-slice(bf16[2,128,704]{1,0,2:T(2,128)(2,1)} %reshape.382.clone.1, bf16[1,128,704]{1,0,2:T(2,128)(2,1)S(1)} %add_convert_fusion.3, s32[]{:T(128)S(6)} %select_n.240, s32[]{:T(128)} %constant.255.clone.1, s32[]{:T(128)} %constant.255.clone.1) | dynamic-update-slice | bytes 360452 | tf_op jit(solution)/shard_map/jit(dynamic_update_index_in_dim)/dynamic_update_slice | solution.py:116
  261.3 9.5 %dynamic_update_slice.154 = bf16[2,128,704]{1,0,2:T(2,128)(2,1)} dynamic-update-slice(bf16[2,128,704]{1,0,2:T(2,128)(2,1)} %dynamic_update_slice.153, bf16[1,128,704]{1,0,2:T(2,128)(2,1)} %collective-permute-done.74, s32[]{:T(128)S(6)} %select_n.241, s32[]{:T(128)} %constant.255.clone.1, s32[]{:T(128)} %constant.255.clone.1) | dynamic-update-slice | bytes 360452 | tf_op jit(solution)/shard_map/jit(dynamic_update_index_in_dim)/dynamic_update_slice | solution.py:117
  272.8 9.2 %dynamic_update_slice.148 = bf16[2,128,704]{1,0,2:T(2,128)(2,1)} dynamic-update-slice(bf16[2,128,704]{1,0,2:T(2,128)(2,1)} %dynamic_update_slice.147, bf16[1,128,704]{1,0,2:T(2,128)(2,1)S(1)} %collective-permute-done.68, s32[]{:T(128)S(6)} %select_n.241, s32[]{:T(128)} %constant.255.clone.1, s32[]{:T(128)} %constant.255.clone.1) | dynamic-update-slice | bytes 360452 | tf_op jit(solution)/shard_map/jit(dynamic_update_index_in_dim)/dynamic_update_slice | solution.py:117
  302.8 19.1 %attention_backward.1 = (bf16[1024,256]{1,0:T(8,128)(2,1)S(1)}, bf16[1024,256]{1,0:T(8,128)(2,1)S(1)}, bf16[1024,256]{1,0:T(8,128)(2,1)S(1)}, bf16[8,256,512]{2,1,0:T(8,128)(2,1)S(1)}) custom-call(s32[3]{0:T(128)S(1)} %copy-done.19, bf16[1024,256]{1,0:T(8,128)(2,1)S(1)} %copy-done.13, bf16[1024,256]{1,0:T(8,128)(2,1)S(1)} %convolution_convert_fusion.7.da_ref, ...), custom_call_target="tpu_custom_call" | custom-call | tf_op jit(solution)/shard_map/attention_backward/pallas_call | solution.py:347
  322.0 17.4 %collective-permute-start.33 = (bf16[128,512]{1,0:T(8,128)(2,1)S(1)}, bf16[128,512]{1,0:T(8,128)(2,1)S(1)}, u32[]{:S(2)}, u32[]{:S(2)}) collective-permute-start(bf16[128,512]{1,0:T(8,128)(2,1)S(1)} %get-tuple-element.78), channel_id=1, source_target_pairs={{0,8},{8,16},{16,24},{24,28},{28,20},{20,12},{12,4},{4,0},{1,9},{9... | collective-permute-start | bytes 393224 | tf_op jit(solution)/shard_map/ppermute | solution.py:67
  341.8 17.7 %collective-permute-done.37 = bf16[128,512]{1,0:T(8,128)(2,1)S(1)} collective-permute-done((bf16[128,512]{1,0:T(8,128)(2,1)S(1)}, bf16[128,512]{1,0:T(8,128)(2,1)S(1)}, u32[]{:S(2)}, u32[]{:S(2)}) %collective-permute-start.37) | collective-permute-done | bytes 131104 | tf_op jit(solution)/shard_map/ppermute | solution.py:67
  360.3 17.3 %collective-permute-start.34 = (bf16[256,512]{1,0:T(8,128)(2,1)}, bf16[256,512]{1,0:T(8,128)(2,1)}, u32[]{:S(2)}, u32[]{:S(2)}) collective-permute-start(bf16[256,512]{1,0:T(8,128)(2,1)} %get-tuple-element.76), channel_id=1, source_target_pairs={{0,8},{8,16},{16,24},{24,28},{28,20},{20,12},{12,4},{4,0},{1,9},{9... | collective-permute-start | bytes 786440 | tf_op jit(solution)/shard_map/ppermute | solution.py:67
  382.9 6.8 %collective-permute-done.38 = bf16[256,512]{1,0:T(8,128)(2,1)} collective-permute-done((bf16[256,512]{1,0:T(8,128)(2,1)S(1)}, bf16[256,512]{1,0:T(8,128)(2,1)}, u32[]{:S(2)}, u32[]{:S(2)}) %collective-permute-start.38) | collective-permute-done | bytes 262176 | tf_op jit(solution)/shard_map/ppermute | solution.py:67
  413.7 4.9 collective-permute-done.40
  458.1 10.4 %collective-permute-done.42 = bf16[256,1024]{1,0:T(8,128)(2,1)S(1)} collective-permute-done((bf16[256,1024]{1,0:T(8,128)(2,1)S(1)}, bf16[256,1024]{1,0:T(8,128)(2,1)S(1)}, u32[]{:S(2)}, u32[]{:S(2)}) %collective-permute-start.42) | collective-permute-done | bytes 524320 | tf_op jit(solution)/shard_map/ppermute | solution.py:39
  470.8 8.1 %collective-permute-done.58 = bf16[256,1024]{1,0:T(8,128)(2,1)S(1)} collective-permute-done((bf16[256,1024]{1,0:T(8,128)(2,1)S(1)}, bf16[256,1024]{1,0:T(8,128)(2,1)S(1)}, u32[]{:S(2)}, u32[]{:S(2)}) %collective-permute-start.58) | collective-permute-done | bytes 524320 | tf_op jit(solution)/shard_map/ppermute | solution.py:39
  481.4 6.7 %collective-permute-done.59 = bf16[4,32,1024]{2,1,0:T(8,128)(2,1)S(1)} collective-permute-done((bf16[4,32,1024]{2,1,0:T(8,128)(2,1)S(1)}, bf16[4,32,1024]{2,1,0:T(8,128)(2,1)S(1)}, u32[]{:S(2)}, u32[]{:S(2)}) %collective-permute-start.59) | collective-permute-done | bytes 262176 | tf_op jit(solution)/shard_map/ppermute | solution.py:39
  489.8 4.8 collective-permute-start.45
  523.8 5.0 collective-permute-done.52
  535.0 5.3 collective-permute-done.54
  540.4 4.9 collective-permute-done.55
  546.9 4.9 collective-permute-done.56
  (514 shorter events, 248.9 us)
Async XLA Ops:
  14.3 20.3 %collective-permute-start.1 = (bf16[256,1024]{1,0:T(8,128)(2,1)}, bf16[256,1024]{1,0:T(8,128)(2,1)S(1)}, u32[]{:S(2)}, u32[]{:S(2)}) collective-permute-start(bf16[256,1024]{1,0:T(8,128)(2,1)} %param.17), channel_id=1, source_target_pairs={{0,2},{1,3},{2,0},{3,1},{4,6},{5,7},{6,4},{7,5},{8,10},{9,11},{10,... | collective-permute-start | bytes 1572872 | tf_op jit(solution)/shard_map/ppermute | solution.py:39
  35.1 23.4 %collective-permute-start.20 = (bf16[256,1024]{1,0:T(8,128)(2,1)S(1)}, bf16[256,1024]{1,0:T(8,128)(2,1)S(1)}, u32[]{:S(2)}, u32[]{:S(2)}) collective-permute-start(bf16[256,1024]{1,0:T(8,128)(2,1)S(1)} %copy-done.49), channel_id=1, source_target_pairs={{0,2},{1,3},{2,0},{3,1},{4,6},{5,7},{6,4},{7,5},{8,10},{9,11},{10,... | collective-permute-start | bytes 1572872 | tf_op jit(solution)/shard_map/ppermute | solution.py:39
  36.9 21.9 %collective-permute-start.21 = (bf16[256,1024]{1,0:T(8,128)(2,1)S(1)}, bf16[256,1024]{1,0:T(8,128)(2,1)S(1)}, u32[]{:S(2)}, u32[]{:S(2)}) collective-permute-start(bf16[256,1024]{1,0:T(8,128)(2,1)S(1)} %copy-done.49), channel_id=1, source_target_pairs={{0,1},{1,0},{2,3},{3,2},{4,5},{5,4},{6,7},{7,6},{8,9},{9,8},{10,11... | collective-permute-start | bytes 1572872 | tf_op jit(solution)/shard_map/ppermute | solution.py:39
  58.5 19.8 %collective-permute-start.28 = (bf16[256,1024]{1,0:T(8,128)(2,1)}, bf16[256,1024]{1,0:T(8,128)(2,1)}, u32[]{:S(2)}, u32[]{:S(2)}) collective-permute-start(bf16[256,1024]{1,0:T(8,128)(2,1)} %fusion.20), channel_id=1, source_target_pairs={{0,2},{1,3},{2,0},{3,1},{4,6},{5,7},{6,4},{7,5},{8,10},{9,11},{10,... | collective-permute-start | bytes 1572872 | tf_op jit(solution)/shard_map/ppermute | solution.py:39
  111.8 61.9 %collective-permute-start.31 = (bf16[2,256,1024]{2,1,0:T(8,128)(2,1)}, bf16[2,256,1024]{2,1,0:T(8,128)(2,1)}, u32[]{:S(2)}, u32[]{:S(2)}) collective-permute-start(bf16[2,256,1024]{2,1,0:T(8,128)(2,1)} %bitcast.26), channel_id=1, source_target_pairs={{0,1},{1,0},{2,3},{3,2},{4,5},{5,4},{6,7},{7,6},{8,9},{9,8},{10,11... | collective-permute-start | bytes 3145736 | tf_op jit(solution)/shard_map/ppermute | solution.py:39
  123.2 31.1 %collective-permute-start.71 = (bf16[4,128,704]{1,0,2:T(4,128)(2,1)}, bf16[4,128,704]{1,0,2:T(4,128)(2,1)}, u32[]{:S(2)}, u32[]{:S(2)}) collective-permute-start(bf16[4,128,704]{1,0,2:T(4,128)(2,1)} %dynamic-slice_bitcast_fusion.1), channel_id=1, source_target_pairs={{0,4},{4,0},{8,12},{12,8},{16,20},{20,16},{24,28},{28,24},{1,5},{5... | collective-permute-start | bytes 2162696 | tf_op jit(solution)/shard_map/ppermute | solution.py:39
  138.1 21.9 %collective-permute-start.65 = (bf16[4,128,704]{1,0,2:T(4,128)(2,1)S(1)}, bf16[4,128,704]{1,0,2:T(4,128)(2,1)S(1)}, u32[]{:S(2)}, u32[]{:S(2)}) collective-permute-start(bf16[4,128,704]{1,0,2:T(4,128)(2,1)S(1)} %dynamic-slice_bitcast_fusion.2), channel_id=1, source_target_pairs={{0,4},{4,0},{8,12},{12,8},{16,20},{20,16},{24,28},{28,24},{1,5},{5... | collective-permute-start | bytes 2162696 | tf_op jit(solution)/shard_map/ppermute | solution.py:39
  144.0 34.0 %collective-permute-start.26 = (bf16[2,256,1024]{2,1,0:T(8,128)(2,1)S(1)}, bf16[2,256,1024]{2,1,0:T(8,128)(2,1)S(1)}, u32[]{:S(2)}, u32[]{:S(2)}) collective-permute-start(bf16[2,256,1024]{2,1,0:T(8,128)(2,1)S(1)} %bitcast.352), channel_id=1, source_target_pairs={{0,1},{1,0},{2,3},{3,2},{4,5},{5,4},{6,7},{7,6},{8,9},{9,8},{10,11... | collective-permute-start | bytes 3145736 | tf_op jit(solution)/shard_map/ppermute | solution.py:39
  144.2 27.2 %collective-permute-start.79 = (bf16[4,88,1024]{2,1,0:T(8,128)(2,1)S(1)}, bf16[4,88,1024]{2,1,0:T(8,128)(2,1)S(1)}, u32[]{:S(2)}, u32[]{:S(2)}) collective-permute-start(bf16[4,88,1024]{2,1,0:T(8,128)(2,1)S(1)} %dynamic-slice_bitcast_fusion), channel_id=1, source_target_pairs={{0,8},{4,12},{8,0},{12,4},{16,24},{20,28},{24,16},{28,20},{1,9},{5... | collective-permute-start | bytes 2162696 | tf_op jit(solution)/shard_map/ppermute | solution.py:39
  156.1 23.6 %collective-permute-start.72 = (bf16[2,128,704]{1,0,2:T(2,128)(2,1)S(1)}, bf16[2,128,704]{1,0,2:T(2,128)(2,1)S(1)}, u32[]{:S(2)}, u32[]{:S(2)}) collective-permute-start(bf16[2,128,704]{1,0,2:T(2,128)(2,1)S(1)} %dynamic-slice_bitcast_fusion.4), channel_id=1, source_target_pairs={{0,8},{4,12},{8,0},{12,4},{16,24},{20,28},{24,16},{28,20},{1,9},{5... | collective-permute-start | bytes 1081352 | tf_op jit(solution)/shard_map/ppermute | solution.py:39
  160.6 37.2 %collective-permute-start.66 = (bf16[2,128,704]{1,0,2:T(2,128)(2,1)S(1)}, bf16[2,128,704]{1,0,2:T(2,128)(2,1)S(1)}, u32[]{:S(2)}, u32[]{:S(2)}) collective-permute-start(bf16[2,128,704]{1,0,2:T(2,128)(2,1)S(1)} %dynamic-slice_bitcast_fusion.5), channel_id=1, source_target_pairs={{0,8},{4,12},{8,0},{12,4},{16,24},{20,28},{24,16},{28,20},{1,9},{5... | collective-permute-start | bytes 1081352 | tf_op jit(solution)/shard_map/ppermute | solution.py:39
  171.6 33.9 %collective-permute-start.80 = (bf16[2,88,1024]{2,1,0:T(8,128)(2,1)S(1)}, bf16[2,88,1024]{2,1,0:T(8,128)(2,1)S(1)}, u32[]{:S(2)}, u32[]{:S(2)}) collective-permute-start(bf16[2,88,1024]{2,1,0:T(8,128)(2,1)S(1)} %dynamic-slice_bitcast_fusion.3), channel_id=1, source_target_pairs={{0,4},{4,0},{8,12},{12,8},{16,20},{20,16},{24,28},{28,24},{1,5},{5... | collective-permute-start | bytes 1081352 | tf_op jit(solution)/shard_map/ppermute | solution.py:39
  176.3 118.9 %collective-permute-start.32 = (bf16[256,1024]{1,0:T(8,128)(2,1)}, bf16[256,1024]{1,0:T(8,128)(2,1)}, u32[]{:S(2)}, u32[]{:S(2)}) collective-permute-start(bf16[256,1024]{1,0:T(8,128)(2,1)} %fusion.26), channel_id=1, source_target_pairs={{0,2},{1,3},{2,0},{3,1},{4,6},{5,7},{6,4},{7,5},{8,10},{9,11},{10,... | collective-permute-start | bytes 1572872 | tf_op jit(solution)/shard_map/ppermute | solution.py:39
  179.4 117.2 %collective-permute-start.27 = (bf16[256,1024]{1,0:T(8,128)(2,1)}, bf16[256,1024]{1,0:T(8,128)(2,1)}, u32[]{:S(2)}, u32[]{:S(2)}) collective-permute-start(bf16[256,1024]{1,0:T(8,128)(2,1)} %fusion.25), channel_id=1, source_target_pairs={{0,2},{1,3},{2,0},{3,1},{4,6},{5,7},{6,4},{7,5},{8,10},{9,11},{10,... | collective-permute-start | bytes 1572872 | tf_op jit(solution)/shard_map/ppermute | solution.py:39
  180.5 46.0 %collective-permute-start.73 = (bf16[1,128,704]{1,0,2:T(2,128)(2,1)S(1)}, bf16[1,128,704]{1,0,2:T(2,128)(2,1)S(1)}, u32[]{:S(2)}, u32[]{:S(2)}) collective-permute-start(bf16[1,128,704]{1,0,2:T(2,128)(2,1)S(1)} %constant_dynamic-slice_fusion.1), channel_id=1, source_target_pairs={{0,16},{4,20},{8,24},{12,28},{16,0},{20,4},{24,8},{28,12},{1,17},{... | collective-permute-start | bytes 540680 | tf_op jit(solution)/shard_map/ppermute | solution.py:39
  199.3 42.7 %collective-permute-start.67 = (bf16[1,128,704]{1,0,2:T(2,128)(2,1)}, bf16[1,128,704]{1,0,2:T(2,128)(2,1)}, u32[]{:S(2)}, u32[]{:S(2)}) collective-permute-start(bf16[1,128,704]{1,0,2:T(2,128)(2,1)} %constant_dynamic-slice_fusion.2), channel_id=1, source_target_pairs={{0,16},{4,20},{8,24},{12,28},{16,0},{20,4},{24,8},{28,12},{1,17},{... | collective-permute-start | bytes 540680 | tf_op jit(solution)/shard_map/ppermute | solution.py:39
  206.3 47.4 %collective-permute-start.81 = (bf16[1,88,1024]{2,1,0:T(8,128)(2,1)}, bf16[1,88,1024]{2,1,0:T(8,128)(2,1)}, u32[]{:S(2)}, u32[]{:S(2)}) collective-permute-start(bf16[1,88,1024]{2,1,0:T(8,128)(2,1)} %constant_dynamic-slice_fusion), channel_id=1, source_target_pairs={{0,16},{4,20},{8,24},{12,28},{16,0},{20,4},{24,8},{28,12},{1,17},{... | collective-permute-start | bytes 540680 | tf_op jit(solution)/shard_map/ppermute | solution.py:39
  226.9 34.3 %collective-permute-start.74 = (bf16[1,128,704]{1,0,2:T(2,128)(2,1)S(1)}, bf16[1,128,704]{1,0,2:T(2,128)(2,1)}, u32[]{:S(2)}, u32[]{:S(2)}) collective-permute-start(bf16[1,128,704]{1,0,2:T(2,128)(2,1)S(1)} %add_convert_fusion.2), channel_id=1, source_target_pairs={{0,16},{4,20},{8,24},{12,28},{16,0},{20,4},{24,8},{28,12},{1,17},{... | collective-permute-start | bytes 540680 | tf_op jit(solution)/shard_map/ppermute | solution.py:39
  243.5 29.3 %collective-permute-start.68 = (bf16[1,128,704]{1,0,2:T(2,128)(2,1)S(1)}, bf16[1,128,704]{1,0,2:T(2,128)(2,1)S(1)}, u32[]{:S(2)}, u32[]{:S(2)}) collective-permute-start(bf16[1,128,704]{1,0,2:T(2,128)(2,1)S(1)} %add_convert_fusion.3), channel_id=1, source_target_pairs={{0,16},{4,20},{8,24},{12,28},{16,0},{20,4},{24,8},{28,12},{1,17},{... | collective-permute-start | bytes 540680 | tf_op jit(solution)/shard_map/ppermute | solution.py:39
  256.2 29.2 %collective-permute-start.82 = (bf16[1,88,1024]{2,1,0:T(8,128)(2,1)}, bf16[1,88,1024]{2,1,0:T(8,128)(2,1)S(1)}, u32[]{:S(2)}, u32[]{:S(2)}) collective-permute-start(bf16[1,88,1024]{2,1,0:T(8,128)(2,1)} %get-tuple-element.52), channel_id=1, source_target_pairs={{0,16},{4,20},{8,24},{12,28},{16,0},{20,4},{24,8},{28,12},{1,17},{... | collective-permute-start | bytes 540680 | tf_op jit(solution)/shard_map/ppermute | solution.py:39
  270.8 109.5 %collective-permute-start.75 = (bf16[2,128,704]{1,0,2:T(2,128)(2,1)}, bf16[2,128,704]{1,0,2:T(2,128)(2,1)}, u32[]{:S(2)}, u32[]{:S(2)}) collective-permute-start(bf16[2,128,704]{1,0,2:T(2,128)(2,1)} %dynamic_update_slice.154), channel_id=1, source_target_pairs={{0,8},{4,12},{8,0},{12,4},{16,24},{20,28},{24,16},{28,20},{1,9},{5... | collective-permute-start | bytes 1081352 | tf_op jit(solution)/shard_map/ppermute | solution.py:39
  282.0 110.9 %collective-permute-start.69 = (bf16[2,128,704]{1,0,2:T(2,128)(2,1)}, bf16[2,128,704]{1,0,2:T(2,128)(2,1)}, u32[]{:S(2)}, u32[]{:S(2)}) collective-permute-start(bf16[2,128,704]{1,0,2:T(2,128)(2,1)} %dynamic_update_slice.148), channel_id=1, source_target_pairs={{0,8},{4,12},{8,0},{12,4},{16,24},{20,28},{24,16},{28,20},{1,9},{5... | collective-permute-start | bytes 1081352 | tf_op jit(solution)/shard_map/ppermute | solution.py:39
  286.1 108.8 %collective-permute-start.83 = (bf16[2,88,1024]{2,1,0:T(8,128)(2,1)}, bf16[2,88,1024]{2,1,0:T(8,128)(2,1)}, u32[]{:S(2)}, u32[]{:S(2)}) collective-permute-start(bf16[2,88,1024]{2,1,0:T(8,128)(2,1)} %constant_dynamic-update-slice_fusion.18), channel_id=1, source_target_pairs={{0,4},{4,0},{8,12},{12,8},{16,20},{20,16},{24,28},{28,24},{1,5},{5... | collective-permute-start | bytes 1081352 | tf_op jit(solution)/shard_map/ppermute | solution.py:39
  322.0 19.9 %collective-permute-start.33 = (bf16[128,512]{1,0:T(8,128)(2,1)S(1)}, bf16[128,512]{1,0:T(8,128)(2,1)S(1)}, u32[]{:S(2)}, u32[]{:S(2)}) collective-permute-start(bf16[128,512]{1,0:T(8,128)(2,1)S(1)} %get-tuple-element.78), channel_id=1, source_target_pairs={{0,8},{8,16},{16,24},{24,28},{28,20},{20,12},{12,4},{4,0},{1,9},{9... | collective-permute-start | bytes 393224 | tf_op jit(solution)/shard_map/ppermute | solution.py:67
  339.3 20.2 %collective-permute-start.37 = (bf16[128,512]{1,0:T(8,128)(2,1)S(1)}, bf16[128,512]{1,0:T(8,128)(2,1)S(1)}, u32[]{:S(2)}, u32[]{:S(2)}) collective-permute-start(bf16[128,512]{1,0:T(8,128)(2,1)S(1)} %get-tuple-element.79), channel_id=1, source_target_pairs={{0,4},{8,0},{16,8},{24,16},{28,24},{20,28},{12,20},{4,12},{1,5},{9... | collective-permute-start | bytes 393224 | tf_op jit(solution)/shard_map/ppermute | solution.py:67
  360.3 22.1 %collective-permute-start.34 = (bf16[256,512]{1,0:T(8,128)(2,1)}, bf16[256,512]{1,0:T(8,128)(2,1)}, u32[]{:S(2)}, u32[]{:S(2)}) collective-permute-start(bf16[256,512]{1,0:T(8,128)(2,1)} %get-tuple-element.76), channel_id=1, source_target_pairs={{0,8},{8,16},{16,24},{24,28},{28,20},{20,12},{12,4},{4,0},{1,9},{9... | collective-permute-start | bytes 786440 | tf_op jit(solution)/shard_map/ppermute | solution.py:67
  380.3 71.6 %collective-permute-start.41 = (bf16[2,256,1024]{2,1,0:T(8,128)(2,1)}, bf16[2,256,1024]{2,1,0:T(8,128)(2,1)}, u32[]{:S(2)}, u32[]{:S(2)}) collective-permute-start(bf16[2,256,1024]{2,1,0:T(8,128)(2,1)} %bitcast.350), channel_id=1, source_target_pairs={{0,1},{1,0},{2,3},{3,2},{4,5},{5,4},{6,7},{7,6},{8,9},{9,8},{10,11... | collective-permute-start | bytes 3145736 | tf_op jit(solution)/shard_map/ppermute | solution.py:39
  382.4 73.1 %collective-permute-start.57 = (bf16[2,256,1024]{2,1,0:T(8,128)(2,1)}, bf16[2,256,1024]{2,1,0:T(8,128)(2,1)}, u32[]{:S(2)}, u32[]{:S(2)}) collective-permute-start(bf16[2,256,1024]{2,1,0:T(8,128)(2,1)} %bitcast.351), channel_id=1, source_target_pairs={{0,1},{1,0},{2,3},{3,2},{4,5},{5,4},{6,7},{7,6},{8,9},{9,8},{10,11... | collective-permute-start | bytes 3145736 | tf_op jit(solution)/shard_map/ppermute | solution.py:39
  395.0 35.5 %collective-permute-start.76 = (bf16[4,128,704]{1,0,2:T(4,128)(2,1)}, bf16[4,128,704]{1,0,2:T(4,128)(2,1)}, u32[]{:S(2)}, u32[]{:S(2)}) collective-permute-start(bf16[4,128,704]{1,0,2:T(4,128)(2,1)} %bitcast.109), channel_id=1, source_target_pairs={{0,4},{4,0},{8,12},{12,8},{16,20},{20,16},{24,28},{28,24},{1,5},{5... | collective-permute-start | bytes 2162696 | tf_op jit(solution)/shard_map/ppermute | solution.py:39
  421.1 25.0 %collective-permute-start.84 = (bf16[4,88,1024]{2,1,0:T(8,128)(2,1)}, bf16[4,88,1024]{2,1,0:T(8,128)(2,1)}, u32[]{:S(2)}, u32[]{:S(2)}) collective-permute-start(bf16[4,88,1024]{2,1,0:T(8,128)(2,1)} %bitcast.123), channel_id=1, source_target_pairs={{0,8},{4,12},{8,0},{12,4},{16,24},{20,28},{24,16},{28,20},{1,9},{5... | collective-permute-start | bytes 2162696 | tf_op jit(solution)/shard_map/ppermute | solution.py:39
  430.4 68.3 %collective-permute-start.49 = (bf16[2,256,1024]{2,1,0:T(8,128)(2,1)}, bf16[2,256,1024]{2,1,0:T(8,128)(2,1)}, u32[]{:S(2)}, u32[]{:S(2)}) collective-permute-start(bf16[2,256,1024]{2,1,0:T(8,128)(2,1)} %bitcast.56), channel_id=1, source_target_pairs={{0,1},{1,0},{2,3},{3,2},{4,5},{5,4},{6,7},{7,6},{8,9},{9,8},{10,11... | collective-permute-start | bytes 3145736 | tf_op jit(solution)/shard_map/ppermute | solution.py:39
  457.2 21.7 %collective-permute-start.58 = (bf16[256,1024]{1,0:T(8,128)(2,1)S(1)}, bf16[256,1024]{1,0:T(8,128)(2,1)S(1)}, u32[]{:S(2)}, u32[]{:S(2)}) collective-permute-start(bf16[256,1024]{1,0:T(8,128)(2,1)S(1)} %fusion.29), channel_id=1, source_target_pairs={{0,2},{1,3},{2,0},{3,1},{4,6},{5,7},{6,4},{7,5},{8,10},{9,11},{10,... | collective-permute-start | bytes 1572872 | tf_op jit(solution)/shard_map/ppermute | solution.py:39
  (137 other events, 1604.5 us)
